TPU v7x, 32 devices: a whole 2x2x4 slice. The times are simulated.
32 devices in a mesh: gx: 8 (over y, x, core), gy: 4 (over z).
Axes of the slice: x: 2, y: 2, z: 4, core: 2. Of those that a mesh axis runs over, the one named last changes fastest.
Arguments:
- velocity: float32 [3, 32, 256, 2048], P(None, None, 'gx', 'gy'), may hold values from -6 to 6
- fiber_points: float32 [256, 3, 128], P(('gx', 'gy')), may hold values from -6 to 6
- stiffness: float32 [256], P(('gx', 'gy')), may hold values from 0.5 to 2
- links: int32 [256, 128], P(('gx', 'gy')), may hold values from 1 to 127
- delta_weights: bfloat16 [256, 8, 128, 512], P(('gx', 'gy')), may hold values from -0.5 to 0.5
- owners: int32 [256, 8, 1], P(('gx', 'gy')), may hold values from 0 to 31; in each aligned block of 64 rows (0 to 63, 64 to 127, ..., all dimensions but the last counted through in order) at most 4 rows name the same one
- patch_slots: int32 [256, 8], P(('gx', 'gy')), may hold values from 0 to 1023
Outputs:
- fluid: float32 [3, 32, 256, 2048], P(None, None, 'gx', 'gy')
- moved_points: float32 [256, 3, 128], P(('gx', 'gy'))
Inputs may be any that keep to these rules, and one draw needn't show every extreme that they name: owners counts devices in the order gx slower, gy faster; among the rows of one device, no owner is named more than 4 times, a bound that some block reaches.
All inputs are finite; a program needn't handle non-finite values.
Results may differ from a plain program's by a relative error of at most 0.0037.
Values may be sent and summed in bfloat16 or wider, within the bound.
A program may use at most 128 MiB of HBM per device.

v0:
```python
import jax
import jax.numpy as jnp
from jax import lax
from jax.sharding import PartitionSpec as P

STEPS = 2


viscosity = 0.1
transport_rate = 0.1
force_step = 0.5
fiber_step = 0.25


def extended_2(cells, sides, width):
    for axis, dim in sides:
        count = lax.axis_size(axis)
        ends = count - 1
        head = lax.slice_in_dim(cells, 0, width, axis=dim)
        tail = lax.slice_in_dim(cells, cells.shape[dim] - width, cells.shape[dim], axis=dim)
        cells = jnp.concatenate(
            [
                lax.ppermute(tail, axis, [(i, (i + 1) % count) for i in range(ends)]),
                cells,
                lax.ppermute(head, axis, [((i + 1) % count, i) for i in range(ends)]),
            ],
            axis=dim,
        )
    return cells


def advance(extended):
    middle = extended[:, :, 1:-1, 1:-1]
    east_cells = extended[:, :, 2:, 1:-1]
    west_cells = extended[:, :, :-2, 1:-1]
    north_cells = extended[:, :, 1:-1, 2:]
    south_cells = extended[:, :, 1:-1, :-2]
    above_cells = jnp.roll(middle, -1, axis=1)
    below_cells = jnp.roll(middle, 1, axis=1)
    laplace = (
        east_cells
        + west_cells
        + north_cells
        + south_cells
        + above_cells
        + below_cells
        - 6.0 * middle
    )
    transport = (
        middle[0:1] * (east_cells - west_cells)
        + middle[1:2] * (north_cells - south_cells)
        + middle[2:3] * (above_cells - below_cells)
    )
    return middle + viscosity * laplace - transport_rate * transport


def shards(velocity, fiber_points, stiffness, links, delta_weights, owners, patch_slots):
    blocks, intersection = (delta_weights.shape[0], delta_weights.shape[1])
    points, patch = (delta_weights.shape[2], delta_weights.shape[3])
    layers, rows, columns = (velocity.shape[1], velocity.shape[2], velocity.shape[3])
    patch_count = layers * rows * columns // patch
    rows_grid, columns_grid = (lax.axis_size("gx"), lax.axis_size("gy"))
    device_count = rows_grid * columns_grid
    entry_total = blocks * intersection
    per_owner = max(2, (2 * entry_total + device_count - 1) // device_count)
    slot_total = device_count * per_owner
    partner = (jnp.arange(points, dtype=jnp.int32)[None, :] + links) % points
    partner_full = jnp.broadcast_to(partner[:, None, :], fiber_points.shape)
    partner_points = jnp.take_along_axis(fiber_points, partner_full, axis=2)
    fiber_force = stiffness[:, None, None] * (partner_points - fiber_points)
    force_bf = fiber_force.astype(jnp.bfloat16)
    contrib = jnp.einsum(
        "bcp,bkpq->bkcq", force_bf, delta_weights, preferred_element_type=jnp.float32
    )
    contrib_flat = contrib.reshape(entry_total, 3, patch)
    owner_list = owners.reshape(entry_total)
    slot_list = patch_slots.reshape(entry_total)
    positions = jnp.arange(entry_total, dtype=jnp.int32)
    earlier = (owner_list[:, None] == owner_list[None, :]) & (
        positions[None, :] < positions[:, None]
    )
    rank = jnp.sum(earlier.astype(jnp.int32), axis=1)
    destination = owner_list * per_owner + rank
    selector = jnp.arange(slot_total, dtype=jnp.int32)[:, None] == destination[None, :]
    outgoing = jnp.einsum(
        "sr,rcq->scq", selector.astype(jnp.float32), contrib_flat, precision=lax.Precision.HIGHEST
    )
    slot_patch = jnp.max(jnp.where(selector, slot_list[None, :], -1), axis=1)
    flat_data, flat_slots = (
        lax.all_to_all(
            outgoing.reshape(device_count, per_owner, 3, patch),
            ("gx", "gy"),
            split_axis=0,
            concat_axis=0,
            tiled=True,
        ),
        lax.all_to_all(
            slot_patch.reshape(device_count, per_owner),
            ("gx", "gy"),
            split_axis=0,
            concat_axis=0,
            tiled=True,
        ),
    )
    received = flat_data.reshape(slot_total, 3, patch)
    received_slots = flat_slots.reshape(slot_total)
    placing = jnp.arange(patch_count, dtype=jnp.int32)[:, None] == received_slots[None, :]
    force_field = jnp.einsum(
        "ps,scq->cpq", placing.astype(jnp.float32), received, precision=lax.Precision.HIGHEST
    )
    moving = velocity + force_step * force_field.reshape(3, layers, rows, columns)
    for step_index in range(STEPS):
        moving = advance(extended_2(moving, (("gx", 2), ("gy", 3)), 1))
    fluid_bf = moving.astype(jnp.bfloat16).reshape(3, patch_count, patch)
    replies = jnp.einsum(
        "ps,cpq->scq", placing.astype(jnp.bfloat16), fluid_bf, preferred_element_type=jnp.float32
    ).astype(jnp.bfloat16)
    returned = lax.all_to_all(
        replies.reshape(device_count, per_owner, 3, patch),
        ("gx", "gy"),
        split_axis=0,
        concat_axis=0,
        tiled=True,
    ).reshape(slot_total, 3, patch)
    picked = jnp.einsum(
        "sr,scq->rcq", selector.astype(jnp.bfloat16), returned, preferred_element_type=jnp.float32
    ).astype(jnp.bfloat16)
    picked = picked.reshape(blocks, intersection, 3, patch)
    interp = jnp.einsum("bkcq,bkpq->bcp", picked, delta_weights, preferred_element_type=jnp.float32)
    return (moving, fiber_points + fiber_step * interp)


def solution(mesh):
    placed = (
        P(None, None, "gx", "gy"),
        P(("gx", "gy"), None, None),
        P(("gx", "gy")),
        P(("gx", "gy"), None),
        P(("gx", "gy"), None, None, None),
        P(("gx", "gy"), None, None),
        P(("gx", "gy"), None),
    )
    return jax.shard_map(
        shards,
        mesh=mesh,
        in_specs=placed,
        out_specs=(P(None, None, "gx", "gy"), P(("gx", "gy"), None, None)),
        check_vma=False,
    )
```

profile of v0, /device:TPU:0, one launch (start us, length us, event | category | flops | bytes accessed | tf_op | source)
XLA Modules:
  0.0 218.6 jit_solution(9418267054246828150)
XLA Ops:
  4.4 7.3 %all-to-all-start.1 = ((s32[32,1,4]{2,1,0:T(1,128)}), s32[32,1,4]{2,1,0:T(1,128)S(1)}, u32[]{:S(2)}, u32[]{:S(2)}) async-start(s32[32,1,4]{2,1,0:T(1,128)} %bitcast.7), calls=%async_computation.1 | async-start | bytes 32768 | tf_op jit(solution)/shard_map/all_to_all | solution.py:97
  12.5 18.5 %gather_fusion = f32[3072]{0:T(1024)S(1)} fusion(f32[8,3,128]{2,0,1:T(8,128)S(1)} %copy-done, s32[3072]{0:T(1024)S(1)} %reshape.82), kind=kCustom, calls=%fused_computation | custom fusion | bytes 61440 | tf_op jit(solution)/shard_map/jit(take_along_axis)/gather | solution.py:69
  31.0 4.6 %fusion.23 = f32[8,3,8,512]{3,1,2,0:T(4,128)S(1)} fusion(bf16[8,8,128,512]{3,2,1,0:T(8,128)(2,1)} %param.11, f32[8,3,128]{2,0,1:T(8,128)S(1)} %copy-done, f32[8,3,128]{2,1,0:T(4,128)S(1)} %reshape.85, s32[8,128]{1,0:T(8,128)S(1)} %get-tuple-element.15, s32[8,128]{1,0:T(8,128)S(1)} %broadcast_add_fusion, f32[8]{0:T(128)S(1)} %copy-done.6, ...), kind=kOutput, calls=%fused_computation.68 | convolution fusion | flops 25190400 | bytes 8815648 | tf_op jit(solution)/shard_map/bcp,bkpq->bkcq/dot_general | solution.py:72
  37.6 5.8 %all-to-all-start = ((f32[32,4,3,512]{3,1,2,0:T(4,128)}), f32[32,4,3,512]{3,1,2,0:T(4,128)S(1)}, u32[]{:S(2)}, u32[]{:S(2)}) async-start(f32[32,4,3,512]{3,1,2,0:T(4,128)} %copy.69), calls=%async_computation | async-start | bytes 1572864 | tf_op jit(solution)/shard_map/all_to_all | solution.py:90
  44.2 18.7 %all-to-all-done = f32[32,4,3,512]{3,1,2,0:T(4,128)S(1)} async-done(((f32[32,4,3,512]{3,1,2,0:T(4,128)}), f32[32,4,3,512]{3,1,2,0:T(4,128)S(1)}, u32[]{:S(2)}, u32[]{:S(2)}) %all-to-all-start) | async-done | bytes 786464 | tf_op jit(solution)/shard_map/all_to_all | solution.py:90
  63.3 4.7 %multiply_bitcast_fusion = f32[3,1024,512]{1,2,0:T(8,128)} fusion(f32[128,3,512]{2,0,1:T(8,128)S(1)} %reshape.77, s32[128]{0:T(128)S(1)} %eq.73), kind=kOutput, calls=%fused_computation.23 | convolution fusion | flops 2417623040 | bytes 7078400 | tf_op jit(solution)/shard_map/ps,scq->cpq/dot_general | solution.py:108
  68.0 6.5 %copy.74 = f32[3,1024,512]{2,1,0:T(8,128)} copy(f32[3,1024,512]{1,2,0:T(8,128)} %multiply_bitcast_fusion) | data formatting | bytes 12582912 | tf_op jit(solution)/shard_map/mul | solution.py:111
  74.5 6.2 %add.91 = f32[3,32,32,512]{3,2,1,0:T(8,128)S(1)} add(f32[3,32,32,512]{3,2,1,0:T(8,128)} %param.7, f32[3,32,32,512]{3,2,1,0:T(8,128)} %bitcast.64) | non-fusion elementwise | flops 1572864 | bytes 18874368 | tf_op jit(solution)/shard_map/add | solution.py:111
  81.1 6.1 %fusion.41 = (f32[3,31,32,512]{3,2,1,0:T(8,128)}, f32[3,31,32,512]{3,2,1,0:T(8,128)}) fusion(f32[3,32,32,512]{3,2,1,0:T(8,128)S(1)} %add.91), kind=kLoop, calls=%fused_computation.92 | loop fusion | bytes 24379392 | tf_op jit(solution)/shard_map/jit(_roll_static)/slice | solution.py:38
  87.2 3.5 %collective-permute-start.1 = (f32[3,32,1,512]{3,2,1,0:T(1,128)S(1)}, f32[3,32,1,512]{3,2,1,0:T(1,128)S(1)}, u32[]{:S(2)}, u32[]{:S(2)}) collective-permute-start(f32[3,32,1,512]{3,2,1,0:T(1,128)S(1)} %get-tuple-element.32), channel_id=1, source_target_pairs={{0,4},{4,8},{8,12},{12,16},{16,20},{20,24},{24,28},{1,5},{5,9},{9,... | collective-permute-start | bytes 589832 | tf_op jit(solution)/shard_map/ppermute | solution.py:23
  91.9 2.9 %slice_bitcast_fusion.5 = (f32[32,32,512]{2,1,0:T(8,128)}, f32[32,32,512]{2,1,0:T(8,128)}, f32[32,32,512]{2,1,0:T(8,128)}) fusion(f32[3,32,32,512]{3,2,1,0:T(8,128)S(1)} %add.91), kind=kLoop, calls=%fused_computation.29 | loop fusion | bytes 12582912 | tf_op jit(solution)/shard_map/mul | solution.py:50
  100.3 2.7 %collective-permute-start.3 = (f32[3,32,34,1]{2,1,3,0:T(8,128)S(1)}, f32[3,32,34,1]{2,1,3,0:T(8,128)S(1)}, u32[]{:S(2)}, u32[]{:S(2)}) collective-permute-start(f32[3,32,34,1]{2,1,3,0:T(8,128)S(1)} %copy.77), channel_id=1, source_target_pairs={{0,1},{1,2},{2,3},{4,5},{5,6},{6,7},{8,9},{9,10},{10,11},{12,13},{... | collective-permute-start | bytes 39176 | tf_op jit(solution)/shard_map/ppermute | solution.py:23
  106.2 2.7 %collective-permute-done.2 = f32[3,32,34,1]{2,1,3,0:T(8,128)S(1)} collective-permute-done((f32[3,32,34,1]{2,1,3,0:T(8,128)S(1)}, f32[3,32,34,1]{2,1,3,0:T(8,128)S(1)}, u32[]{:S(2)}, u32[]{:S(2)}) %collective-permute-start.2) | collective-permute-done | bytes 13088 | tf_op jit(solution)/shard_map/ppermute | solution.py:25
  111.8 23.8 %multiply_subtract_fusion.1 = f32[3,32,32,512]{3,2,1,0:T(8,128)S(1)} fusion(f32[3,32,32,512]{3,2,1,0:T(8,128)} %copy-done.2, f32[3,31,32,512]{3,2,1,0:T(8,128)} %get-tuple-element.35, f32[3,1,32,512]{3,2,1,0:T(8,128)} %get-tuple-element.37, f32[3,1,32,512]{3,2,1,0:T(8,128)} %get-tuple-element.36, f32[3,31,32,512]{3,2,1,0:T(8,128)} %get-tuple-element.34, ...), kind=kLoop, calls=%fused_computation.22 | loop fusion | flops 45613056 | bytes 31876608 | tf_op jit(solution)/shard_map/sub | solution.py:54
  136.0 6.0 %fusion.38 = (f32[3,31,32,512]{3,2,1,0:T(8,128)}, f32[3,31,32,512]{3,2,1,0:T(8,128)}) fusion(f32[3,32,32,512]{3,2,1,0:T(8,128)S(1)} %multiply_subtract_fusion.1), kind=kLoop, calls=%fused_computation.89 | loop fusion | bytes 24379392 | tf_op jit(solution)/shard_map/jit(_roll_static)/slice | solution.py:38
  141.9 3.8 %collective-permute-start.5 = (f32[3,32,1,512]{3,2,1,0:T(1,128)S(1)}, f32[3,32,1,512]{3,2,1,0:T(1,128)S(1)}, u32[]{:S(2)}, u32[]{:S(2)}) collective-permute-start(f32[3,32,1,512]{3,2,1,0:T(1,128)S(1)} %get-tuple-element.20), channel_id=1, source_target_pairs={{0,4},{4,8},{8,12},{12,16},{16,20},{20,24},{24,28},{1,5},{5,9},{9,... | collective-permute-start | bytes 589832 | tf_op jit(solution)/shard_map/ppermute | solution.py:23
  147.1 2.9 %slice_bitcast_fusion.2 = (f32[32,32,512]{2,1,0:T(8,128)}, f32[32,32,512]{2,1,0:T(8,128)}, f32[32,32,512]{2,1,0:T(8,128)}) fusion(f32[3,32,32,512]{3,2,1,0:T(8,128)S(1)} %multiply_subtract_fusion.1), kind=kLoop, calls=%fused_computation.26 | loop fusion | bytes 12582912 | tf_op jit(solution)/shard_map/mul | solution.py:50
  150.0 2.8 %pad_maximum_fusion.22 = (f32[3,32,34,1]{3,2,1,0:T(8,128)}, f32[3,32,34,1]{3,2,1,0:T(8,128)}) fusion(f32[3,32,1,512]{3,2,1,0:T(1,128)S(1)} %collective-permute-done.4, f32[3,32,32,512]{3,2,1,0:T(8,128)S(1)} %multiply_subtract_fusion.1, f32[3,32,1,512]{3,2,1,0:T(1,128)S(1)} %collective-permute-done.5), kind=kLoop, calls=%fused_computation.32 | loop fusion | flops 13056 | bytes 6710784 | tf_op jit(solution)/shard_map/slice | solution.py:19
  152.8 2.5 %copy.79 = f32[3,32,34,1]{2,1,3,0:T(8,128)S(1)} copy(f32[3,32,34,1]{3,2,1,0:T(8,128)} %get-tuple-element.16) | data formatting | bytes 26112 | tf_op jit(solution)/shard_map/slice | solution.py:19
  157.5 3.3 %collective-permute-start.7 = (f32[3,32,34,1]{2,1,3,0:T(8,128)S(1)}, f32[3,32,34,1]{2,1,3,0:T(8,128)S(1)}, u32[]{:S(2)}, u32[]{:S(2)}) collective-permute-start(f32[3,32,34,1]{2,1,3,0:T(8,128)S(1)} %copy.81), channel_id=1, source_target_pairs={{0,1},{1,2},{2,3},{4,5},{5,6},{6,7},{8,9},{9,10},{10,11},{12,13},{... | collective-permute-start | bytes 39176 | tf_op jit(solution)/shard_map/ppermute | solution.py:23
  163.2 3.6 %collective-permute-done.6 = f32[3,32,34,1]{2,1,3,0:T(8,128)S(1)} collective-permute-done((f32[3,32,34,1]{2,1,3,0:T(8,128)S(1)}, f32[3,32,34,1]{2,1,3,0:T(8,128)S(1)}, u32[]{:S(2)}, u32[]{:S(2)}) %collective-permute-start.6) | collective-permute-done | bytes 13088 | tf_op jit(solution)/shard_map/ppermute | solution.py:25
  171.1 21.3 %fusion.36 = (bf16[3,32,32,512]{3,2,1,0:T(8,128)(2,1)S(1)}, f32[3,32,32,512]{3,2,1,0:T(8,128)}) fusion(f32[32,32,512]{2,1,0:T(8,128)} %get-tuple-element.27, f32[32,32,512]{2,1,0:T(8,128)} %get-tuple-element.28, f32[32,32,512]{2,1,0:T(8,128)S(1)} %copy-done.3, f32[3,32,32,512]{3,2,1,0:T(8,128)} %copy-done.1, f32[3,31,32,512]{3,2,1,0:T(8,128)} %get-tuple-element.23, ...), kind=kLoop, calls=%fused_computation.87 | loop fusion | flops 47185920 | bytes 35022336 | tf_op jit(solution)/shard_map/convert_element_type | solution.py:114
  193.3 18.6 %all_to_all.19 = bf16[32,4,3,512]{3,1,2,0:T(4,128)(2,1)S(1)} all-to-all(bf16[32,4,3,512]{3,1,2,0:T(4,128)(2,1)S(1)} %copy.83), channel_id=1, replica_groups=mesh['gx'=8,'gy'=4] {'gx','gy'}, dimensions={0} | all-to-all | bytes 786432 | tf_op jit(solution)/shard_map/all_to_all | solution.py:118
  212.3 5.7 %fusion.2 = f32[8,3,128]{2,1,0:T(4,128)S(1)} fusion(bf16[8,8,128,512]{3,2,1,0:T(8,128)(2,1)} %param.11, bf16[8,8,3,512]{3,1,0,2:T(8,128)(2,1)S(1)} %fusion, f32[8,3,128]{2,0,1:T(8,128)S(1)} %copy-done), kind=kOutput, calls=%fused_computation.41 | convolution fusion | flops 25171968 | bytes 8609792 | tf_op jit(solution)/shard_map/bkcq,bkpq->bcp/dot_general | solution.py:129
  (64 shorter events, 33.4 us)
Async XLA Ops:
  0.6 11.8 %copy-start = (f32[8,3,128]{2,0,1:T(8,128)S(1)}, f32[8,3,128]{2,0,1:T(8,128)}, u32[]{:S(2)}) copy-start(f32[8,3,128]{2,0,1:T(8,128)} %param.8) | copy-start | bytes 36868
  4.4 33.2 %all-to-all-start.1 = ((s32[32,1,4]{2,1,0:T(1,128)}), s32[32,1,4]{2,1,0:T(1,128)S(1)}, u32[]{:S(2)}, u32[]{:S(2)}) async-start(s32[32,1,4]{2,1,0:T(1,128)} %bitcast.7), calls=%async_computation.1 | async-start | bytes 32768 | tf_op jit(solution)/shard_map/all_to_all | solution.py:97
  12.5 18.5 %copy-start.6 = (f32[8]{0:T(128)S(1)}, f32[8]{0:T(128)}, u32[]{:S(2)}) copy-start(f32[8]{0:T(128)} %param.9) | copy-start | bytes 100
  37.6 25.3 %all-to-all-start = ((f32[32,4,3,512]{3,1,2,0:T(4,128)}), f32[32,4,3,512]{3,1,2,0:T(4,128)S(1)}, u32[]{:S(2)}, u32[]{:S(2)}) async-start(f32[32,4,3,512]{3,1,2,0:T(4,128)} %copy.69), calls=%async_computation | async-start | bytes 1572864 | tf_op jit(solution)/shard_map/all_to_all | solution.py:90
  80.6 14.2 %copy-start.2 = (f32[3,32,32,512]{3,2,1,0:T(8,128)}, f32[3,32,32,512]{3,2,1,0:T(8,128)S(1)}, u32[]{:S(2)}) copy-start(f32[3,32,32,512]{3,2,1,0:T(8,128)S(1)} %add.91) | copy-start | bytes 18874372
  87.2 7.7 %collective-permute-start.1 = (f32[3,32,1,512]{3,2,1,0:T(1,128)S(1)}, f32[3,32,1,512]{3,2,1,0:T(1,128)S(1)}, u32[]{:S(2)}, u32[]{:S(2)}) collective-permute-start(f32[3,32,1,512]{3,2,1,0:T(1,128)S(1)} %get-tuple-element.32), channel_id=1, source_target_pairs={{0,4},{4,8},{8,12},{12,16},{16,20},{20,24},{24,28},{1,5},{5,9},{9,... | collective-permute-start | bytes 589832 | tf_op jit(solution)/shard_map/ppermute | solution.py:23
  90.6 4.2 %collective-permute-start = (f32[3,32,1,512]{3,2,1,0:T(1,128)S(1)}, f32[3,32,1,512]{3,2,1,0:T(1,128)S(1)}, u32[]{:S(2)}, u32[]{:S(2)}) collective-permute-start(f32[3,32,1,512]{3,2,1,0:T(1,128)S(1)} %get-tuple-element.33), channel_id=1, source_target_pairs={{4,0},{8,4},{12,8},{16,12},{20,16},{24,20},{28,24},{5,1},{9,5},{13... | collective-permute-start | bytes 589832 | tf_op jit(solution)/shard_map/ppermute | solution.py:25
  94.8 2.4 %copy-start.4 = (f32[3,32,1,512]{3,2,1,0:T(1,128)}, f32[3,32,1,512]{3,2,1,0:T(1,128)S(1)}, u32[]{:S(2)}) copy-start(f32[3,32,1,512]{3,2,1,0:T(1,128)S(1)} %collective-permute-done.1) | copy-start | bytes 589828
  94.8 2.4 %copy-start.5 = (f32[3,32,1,512]{3,2,1,0:T(1,128)}, f32[3,32,1,512]{3,2,1,0:T(1,128)S(1)}, u32[]{:S(2)}) copy-start(f32[3,32,1,512]{3,2,1,0:T(1,128)S(1)} %collective-permute-done) | copy-start | bytes 589828
  100.3 9.5 %collective-permute-start.3 = (f32[3,32,34,1]{2,1,3,0:T(8,128)S(1)}, f32[3,32,34,1]{2,1,3,0:T(8,128)S(1)}, u32[]{:S(2)}, u32[]{:S(2)}) collective-permute-start(f32[3,32,34,1]{2,1,3,0:T(8,128)S(1)} %copy.77), channel_id=1, source_target_pairs={{0,1},{1,2},{2,3},{4,5},{5,6},{6,7},{8,9},{9,10},{10,11},{12,13},{... | collective-permute-start | bytes 39176 | tf_op jit(solution)/shard_map/ppermute | solution.py:23
  102.9 6.0 %collective-permute-start.2 = (f32[3,32,34,1]{2,1,3,0:T(8,128)S(1)}, f32[3,32,34,1]{2,1,3,0:T(8,128)S(1)}, u32[]{:S(2)}, u32[]{:S(2)}) collective-permute-start(f32[3,32,34,1]{2,1,3,0:T(8,128)S(1)} %copy.75), channel_id=1, source_target_pairs={{1,0},{2,1},{3,2},{5,4},{6,5},{7,6},{9,8},{10,9},{11,10},{13,12},{... | collective-permute-start | bytes 39176 | tf_op jit(solution)/shard_map/ppermute | solution.py:25
  135.6 14.4 %copy-start.1 = (f32[3,32,32,512]{3,2,1,0:T(8,128)}, f32[3,32,32,512]{3,2,1,0:T(8,128)S(1)}, u32[]{:S(2)}) copy-start(f32[3,32,32,512]{3,2,1,0:T(8,128)S(1)} %multiply_subtract_fusion.1) | copy-start | bytes 18874372
  141.9 8.0 %collective-permute-start.5 = (f32[3,32,1,512]{3,2,1,0:T(1,128)S(1)}, f32[3,32,1,512]{3,2,1,0:T(1,128)S(1)}, u32[]{:S(2)}, u32[]{:S(2)}) collective-permute-start(f32[3,32,1,512]{3,2,1,0:T(1,128)S(1)} %get-tuple-element.20), channel_id=1, source_target_pairs={{0,4},{4,8},{8,12},{12,16},{16,20},{20,24},{24,28},{1,5},{5,9},{9,... | collective-permute-start | bytes 589832 | tf_op jit(solution)/shard_map/ppermute | solution.py:23
  145.8 4.2 %collective-permute-start.4 = (f32[3,32,1,512]{3,2,1,0:T(1,128)S(1)}, f32[3,32,1,512]{3,2,1,0:T(1,128)S(1)}, u32[]{:S(2)}, u32[]{:S(2)}) collective-permute-start(f32[3,32,1,512]{3,2,1,0:T(1,128)S(1)} %get-tuple-element.21), channel_id=1, source_target_pairs={{4,0},{8,4},{12,8},{16,12},{20,16},{24,20},{28,24},{5,1},{9,5},{13... | collective-permute-start | bytes 589832 | tf_op jit(solution)/shard_map/ppermute | solution.py:25
  152.8 18.3 %copy-start.3 = (f32[32,32,512]{2,1,0:T(8,128)S(1)}, f32[32,32,512]{2,1,0:T(8,128)}, u32[]{:S(2)}) copy-start(f32[32,32,512]{2,1,0:T(8,128)} %get-tuple-element.26) | copy-start | bytes 6291460
  157.5 11.5 %collective-permute-start.7 = (f32[3,32,34,1]{2,1,3,0:T(8,128)S(1)}, f32[3,32,34,1]{2,1,3,0:T(8,128)S(1)}, u32[]{:S(2)}, u32[]{:S(2)}) collective-permute-start(f32[3,32,34,1]{2,1,3,0:T(8,128)S(1)} %copy.81), channel_id=1, source_target_pairs={{0,1},{1,2},{2,3},{4,5},{5,6},{6,7},{8,9},{9,10},{10,11},{12,13},{... | collective-permute-start | bytes 39176 | tf_op jit(solution)/shard_map/ppermute | solution.py:23
  160.9 6.0 %collective-permute-start.6 = (f32[3,32,34,1]{2,1,3,0:T(8,128)S(1)}, f32[3,32,34,1]{2,1,3,0:T(8,128)S(1)}, u32[]{:S(2)}, u32[]{:S(2)}) collective-permute-start(f32[3,32,34,1]{2,1,3,0:T(8,128)S(1)} %copy.79), channel_id=1, source_target_pairs={{1,0},{2,1},{3,2},{5,4},{6,5},{7,6},{9,8},{10,9},{11,10},{13,12},{... | collective-permute-start | bytes 39176 | tf_op jit(solution)/shard_map/ppermute | solution.py:25
where the time goes:
time: 220 us; the launch traced here: 219 us
  local copies, waits for them, and re-layouts  66.4 us (30%)
  other arithmetic  59.4 us (27%)
  starting transfers between devices  31.8 us (14%)
  waiting for transfers between devices  25 us (11%)
  blocking collectives  18.6 us (8%)
  matrix products  16.5 us (8%)
    sub x1, other arithmetic, advance(): return middle + viscosity * laplace - transport_rate * transport  23.8 us
    convert_element_type x1, other arithmetic, shards(): fluid_bf = moving.astype(jnp.bfloat16).reshape(3, patch_count, patch)  21.3 us
    all_to_all x1, waiting for transfers between devices, shards(): lax.all_to_all(outgoing.reshape(device_count, per_owner, 3, patch), ('gx'...  18.7 us
    all_to_all x1, blocking collectives, shards(): lax.all_to_all(replies.reshape(device_count, per_owner, 3, patch), ('gx',...  18.6 us
    gather x3, local copies, waits for them, and re-layouts, shards(): partner_points = jnp.take_along_axis(fiber_points, partner_full, axis=2)  18.5 us
    slice x4, local copies, waits for them, and re-layouts, advance(): above_cells = jnp.roll(middle, -1, axis=1)  14.9 us
    ppermute x4, starting transfers between devices, extended_2(): lax.ppermute(tail, axis, [(i, (i + 1) % count) for i in range(ends)])  13.3 us
    all_to_all x1, starting transfers between devices, shards(): lax.all_to_all(slot_patch.reshape(device_count, per_owner), ('gx', 'gy'),...  7.33 us
  transfers between devices with their start and end apart: 10, of which 3 were waited for; matrix products, arithmetic and copies ran while one was open for 17% of the time, Pallas kernels for 0%

commit v1 on v0

v1 whole, which is shorter than its diff:
```python
import functools

import jax
import jax.numpy as jnp
from jax import lax
from jax.experimental import pallas as pl
from jax.experimental.pallas import tpu as pltpu
from jax.sharding import PartitionSpec as P

STEPS = 2
viscosity = 0.1
transport_rate = 0.1
force_step = 0.5
fiber_step = 0.25

F32 = jnp.float32
BF16 = jnp.bfloat16
I32 = jnp.int32
LANES = 128
MESH = pl.DeviceIdType.MESH
VMEM = pl.BlockSpec(memory_space=pltpu.VMEM)
ANY = pl.BlockSpec(memory_space=pl.ANY)
SMEM = pl.BlockSpec(memory_space=pltpu.SMEM)


def iota(shape, dim):
    return lax.broadcasted_iota(I32, shape, dim)


def to_column(row):
    n = row.shape[1]
    return jnp.sum(jnp.where(iota((n, n), 0) == iota((n, n), 1), row, 0), axis=1, keepdims=True)


def slot_row(owner_row, owner_column, devices):
    n = owner_row.shape[1]
    same = (owner_column == owner_row) & (iota((n, n), 0) < iota((n, n), 1))
    rank = jnp.sum(jnp.where(same, 1, 0), axis=0, keepdims=True)
    return rank * devices + owner_row


def slot_column(owner_row, owner_column, devices):
    n = owner_row.shape[1]
    same = (owner_column == owner_row) & (iota((n, n), 1) < iota((n, n), 0))
    rank = jnp.sum(jnp.where(same, 1, 0), axis=1, keepdims=True)
    return rank * devices + owner_column


def spread_kernel(
    devices, per_owner, points_ref, stiffness_ref, links_ref, owners_ref, slots_ref, weights_ref,
    out_ref, table_ref, force_ref, contrib_ref, stage_ref,
):
    b = pl.program_id(0)
    blocks = pl.num_programs(0)
    k, points, patch = weights_ref.shape[1:]

    @pl.when(b == 0)
    def _():
        partner = lax.rem(iota(links_ref.shape, 1) + links_ref[...], points)
        for c in range(3):
            here = points_ref[:, c, :]
            there = jnp.take_along_axis(here, partner, axis=1)
            force_ref[c] = stiffness_ref[...] * (there - here)

    diagonal = iota((k, k * points), 0) == iota((k, k * points), 1) // points
    rows = []
    for c in range(3):
        row = force_ref[c, pl.ds(b, 1), :]
        rows.append(jnp.where(diagonal, jnp.concatenate([row] * k, axis=1), 0.0))
    rows.append(jnp.zeros_like(rows[0]))
    left = jnp.concatenate(rows, axis=0).astype(BF16)
    right = weights_ref[0].reshape(k * points, patch)
    result = jnp.dot(left, right, preferred_element_type=F32)
    for c in range(3):
        contrib_ref[c, pl.ds(pl.multiple_of(b * k, k), k), :] = result[c * k:(c + 1) * k]

    @pl.when(b == blocks - 1)
    def _():
        owner_row = owners_ref[...]
        owner_column = to_column(owner_row)
        places = slot_row(owner_row, owner_column, devices)
        total = devices * per_owner
        chosen = iota((total, places.shape[1]), 0) == places
        selector = chosen.astype(F32).astype(BF16)
        tiles = patch // LANES
        width = 3 * tiles * per_owner
        for c in range(3):
            packed = jnp.dot(selector, contrib_ref[c].astype(BF16), preferred_element_type=F32)
            for p in range(per_owner):
                for t in range(tiles):
                    stage_ref[pl.ds(p * 3 * tiles + c * tiles + t, devices, stride=width), :] = (
                        packed[p * devices:(p + 1) * devices, t * LANES:(t + 1) * LANES]
                    )
        out_ref[...] = stage_ref[...].reshape(out_ref.shape).astype(BF16)
        column = jnp.max(jnp.where(chosen, slots_ref[...], -1), axis=1, keepdims=True)
        lane = iota((devices, LANES), 1)
        table = jnp.full((devices, LANES), -1, I32)
        for p in range(per_owner):
            table = jnp.where(lane == p, column[p * devices:(p + 1) * devices], table)
        for d in range(devices):
            table_ref[d] = table[d:d + 1]


def greet(others):
    barrier = pltpu.get_barrier_semaphore()
    for other in others:
        pl.semaphore_signal(barrier, inc=1, device_id=other, device_id_type=MESH)
    pl.semaphore_wait(barrier, len(others))


def swap_kernel(rows, columns, count, *refs):
    ins, outs = refs[:count], refs[count:2 * count]
    send_sem, recv_sem, own_sem = refs[2 * count:]
    devices = rows * columns
    me = lax.axis_index("gx") * columns + lax.axis_index("gy")

    def place(d):
        return (d // columns, lax.rem(d, columns))

    barrier = pltpu.get_barrier_semaphore()

    def hello(off, carry):
        other = lax.rem(me + off, devices)
        pl.semaphore_signal(barrier, inc=1, device_id=place(other), device_id_type=MESH)
        return carry

    lax.fori_loop(1, devices, hello, 0)
    pl.semaphore_wait(barrier, devices - 1)

    def copy(n, off):
        other = lax.rem(me + off, devices)
        return pltpu.make_async_remote_copy(
            src_ref=ins[n].at[other], dst_ref=outs[n].at[me],
            send_sem=send_sem.at[n, off], recv_sem=recv_sem.at[n, off],
            device_id=place(other), device_id_type=MESH,
        )

    def start(off, carry):
        for n in range(count):
            copy(n, off).start()
        return carry

    def finish(off, carry):
        for n in range(count):
            copy(n, off).wait()
        return carry

    lax.fori_loop(1, devices, start, 0)
    for n in range(count):
        pltpu.make_async_copy(ins[n].at[me], outs[n].at[me], own_sem.at[n]).start()
    for n in range(count):
        pltpu.make_async_copy(ins[n].at[me], outs[n].at[me], own_sem.at[n]).wait()
    lax.fori_loop(1, devices, finish, 0)


def swap(arrays, rows, columns, collective_id):
    devices = rows * columns
    count = len(arrays)
    return pl.pallas_call(
        functools.partial(swap_kernel, rows, columns, count),
        out_shape=[jax.ShapeDtypeStruct(a.shape, a.dtype) for a in arrays],
        in_specs=[VMEM] * count,
        out_specs=[VMEM] * count,
        scratch_shapes=[
            pltpu.SemaphoreType.DMA((count, devices)),
            pltpu.SemaphoreType.DMA((count, devices)),
            pltpu.SemaphoreType.DMA((count,)),
        ],
        compiler_params=pltpu.CompilerParams(collective_id=collective_id, has_side_effects=True),
    )(*arrays)


def unpack(stage_ref, devices, per_owner, tiles, c):
    width = 3 * tiles * per_owner
    rows = []
    for p in range(per_owner):
        rows.append(jnp.concatenate(
            [stage_ref[pl.ds(p * 3 * tiles + c * tiles + t, devices, stride=width), :]
             for t in range(tiles)], axis=1))
    return jnp.concatenate(rows, axis=0)


def add_kernel(
    devices, per_owner, received_ref, table_ref, velocity_ref,
    u_ref, sides_ref, ends_ref, corners_ref, stage_ref, force_ref, side_ref, corner_ref,
):
    i = pl.program_id(0)
    steps = pl.num_programs(0)
    _, depth, rows, columns = velocity_ref.shape
    tiles = columns // LANES
    total = devices * per_owner
    layers = depth * steps
    cells = depth * rows

    @pl.when(i == 0)
    def _():
        stage_ref[...] = received_ref[...].astype(F32).reshape(stage_ref.shape)
        for c in range(3):
            force_ref[c] = unpack(stage_ref, devices, per_owner, tiles, c).astype(BF16)
        corner_ref[...] = jnp.zeros_like(corner_ref)

    row = jnp.zeros((1, total), I32)
    for p in range(per_owner):
        column = table_ref[:, 0, :][:, p:p + 1]
        spot = iota((devices, total), 1) == p * devices + iota((devices, total), 0)
        row = row + jnp.sum(jnp.where(spot, column, 0), axis=0, keepdims=True)
    placing = (iota((cells, total), 0) + i * cells == row).astype(F32).astype(BF16)
    r16, c16 = iota((16, columns), 0), iota((16, columns), 1)
    pick = (r16 < 2) & (c16 == r16) | (r16 >= 2) & (r16 < 4) & (c16 == columns - 4 + r16)
    pick = pick.astype(F32).astype(BF16)
    cell, want = iota((cells, LANES), 0), iota((cells, LANES), 1)
    z, x = cell // rows + i * depth, lax.rem(cell, rows)
    edge = (x == 0) & (want == z) | (x == rows - 1) & (want == layers + z)
    edge = edge.astype(F32).astype(BF16)
    for c in range(3):
        push = jnp.dot(placing, force_ref[c], preferred_element_type=F32)
        u = velocity_ref[c] + force_step * push.reshape(depth, rows, columns)
        u_ref[c] = u
        for side in range(2):
            for r in range(2):
                x = r + side * (rows - 2)
                side_ref[side, c, r, pl.ds(pl.multiple_of(i * depth, depth), depth), :] = u_ref[c, :, x, :]
        flat = u.reshape(cells, columns).astype(BF16)
        ends = lax.dot_general(
            pick, flat, (((1,), (1,)), ((), ())), preferred_element_type=F32).astype(BF16)
        ends_ref[c] = ends
        corner_ref[c] += jnp.dot(ends, edge, preferred_element_type=F32)

    @pl.when(i == steps - 1)
    def _():
        sides_ref[...] = side_ref[...].astype(BF16)
        corners_ref[...] = corner_ref[...].astype(BF16)


def halo_kernel(
    rows, columns, sides_ref, ends_ref, corners_ref,
    sides_out, ends_out, corners_out, send_sem, recv_sem,
):
    gx, gy = lax.axis_index("gx"), lax.axis_index("gy")
    east, west = lax.rem(gx + 1, rows), lax.rem(gx + rows - 1, rows)
    north, south = lax.rem(gy + 1, columns), lax.rem(gy + columns - 1, columns)
    others = [
        (west, gy), (east, gy), (gx, south), (gx, north),
        (west, south), (west, north), (east, south), (east, north),
    ]
    greet(others)
    pairs = [
        (sides_ref.at[0], sides_out.at[1]), (sides_ref.at[1], sides_out.at[0]),
        (ends_ref, ends_out.at[1]), (ends_ref, ends_out.at[0]),
        (corners_ref, corners_out.at[3]), (corners_ref, corners_out.at[2]),
        (corners_ref, corners_out.at[1]), (corners_ref, corners_out.at[0]),
    ]
    copies = [
        pltpu.make_async_remote_copy(
            src_ref=source, dst_ref=target, send_sem=send_sem.at[n], recv_sem=recv_sem.at[n],
            device_id=other, device_id_type=MESH)
        for n, ((source, target), other) in enumerate(zip(pairs, others))
    ]
    for copy in copies:
        copy.start()
    for copy in copies:
        copy.wait()


def sweep(mid, east, west, north, south, above, below):
    r = transport_rate
    coefficients = [(viscosity - r * m, viscosity + r * m) for m in mid]
    keep = 1.0 - 6.0 * viscosity
    out = []
    for c in range(3):
        v = keep * mid[c]
        for (ahead, behind), (front, back) in zip(
            coefficients, ((east, west), (north, south), (above, below))
        ):
            v = v + (ahead * front[c] + behind * back[c])
        out.append(v)
    return out


def sweeps_kernel(
    devices, per_owner, chunk, flags_ref, sides_ref, ends_ref, corners_ref, table_ref, u_ref,
    fluid_ref, replies_ref, first_ref, second_ref, last_ref, side_ref, stage_ref, sum_ref,
    in_sem, out_sem,
):
    _, layers, rows, columns = u_ref.shape
    tiles = columns // LANES
    total = devices * per_owner
    chunks = layers // chunk

    def load(n):
        span = pl.ds(n * chunk, chunk)
        return pltpu.make_async_copy(
            u_ref.at[:, span], first_ref.at[:, span, 0:rows, 0:columns], in_sem.at[n])

    for n in range(chunks):
        load(n).start()

    has = [flags_ref[n] > 0 for n in range(4)]
    for side in range(2):
        side_ref[side, :, :, :, 0:columns] = jnp.where(has[side], sides_ref[side].astype(F32), 0.0)
        side_ref[side, :, :, :, columns:] = jnp.zeros((3, 2, layers, LANES), F32)
    r16, l16 = iota((16, LANES), 0), iota((16, LANES), 1)
    zero = jnp.zeros((16, LANES), F32)
    from_south = (r16 >= 2) & (r16 < 4) & (l16 == LANES - 4 + r16)
    from_north = (r16 < 2) & (l16 == r16)
    south_pick = jnp.where(has[2], from_south.astype(F32), zero).astype(BF16)
    north_pick = jnp.where(has[3], from_north.astype(F32), zero).astype(BF16)

    def expand(values, pick):
        return lax.dot_general(
            values, pick, (((0,), (0,)), ((), ())), preferred_element_type=F32)

    for c in range(3):
        band = expand(ends_ref[0, c], south_pick) + expand(ends_ref[1, c], north_pick)
        first_ref[c, :, 0:rows, columns:] = band.reshape(layers, rows, LANES)
        low = expand(corners_ref[0, c], south_pick) + expand(corners_ref[1, c], north_pick)
        high = expand(corners_ref[2, c], south_pick) + expand(corners_ref[3, c], north_pick)
        side_ref[0, c, 1, :, columns:] = jnp.where(has[0], low[layers:2 * layers], 0.0)
        side_ref[1, c, 0, :, columns:] = jnp.where(has[1], high[0:layers], 0.0)

    r8 = iota((8, columns + LANES), 0)

    def border(z, carry):
        for c in range(3):
            tile = jnp.zeros((8, columns + LANES), F32)
            for place, side, r in ((0, 1, 0), (1, 1, 1), (6, 0, 0), (7, 0, 1)):
                tile = jnp.where(r8 == place, side_ref[side, c, r, pl.ds(z, 1), :], tile)
            first_ref[c, pl.ds(z, 1), rows:, :] = tile[None]
        return carry

    lax.fori_loop(0, layers, border, 0)
    for n in range(chunks):
        load(n).wait()

    tall, wide = rows + 8, columns + LANES
    row, lane = iota((tall, wide), 0), iota((tall, wide), 1)
    keep = (
        (row < rows) | ((row == rows) & has[1]) | ((row == tall - 1) & has[0])
    ) & ((lane < columns) | ((lane == columns) & has[3]) | ((lane == wide - 1) & has[2]))

    def plane(ref, z):
        return [ref[c, z] for c in range(3)]

    def step_one(z, carry):
        up, down = lax.rem(z + 1, layers), lax.rem(z + layers - 1, layers)
        mid = plane(first_ref, z)
        east = [pltpu.roll(m, tall - 1, 0) for m in mid]
        west = [pltpu.roll(m, 1, 0) for m in mid]
        north = [pltpu.roll(m, wide - 1, 1) for m in mid]
        south = [pltpu.roll(m, 1, 1) for m in mid]
        new = sweep(mid, east, west, north, south, plane(first_ref, up), plane(first_ref, down))
        for c in range(3):
            second_ref[c, z] = jnp.where(keep, new[c], 0.0)
        return carry

    lax.fori_loop(0, layers, step_one, 0)

    def inner(values):
        return [v[0:rows, 0:columns] for v in values]

    def step_two(z, carry):
        up, down = lax.rem(z + 1, layers), lax.rem(z + layers - 1, layers)
        mid = plane(second_ref, z)
        east = inner([pltpu.roll(m[:, 0:columns], tall - 1, 0) for m in mid])
        west = inner([pltpu.roll(m[:, 0:columns], 1, 0) for m in mid])
        north = inner([pltpu.roll(m[0:rows], wide - 1, 1) for m in mid])
        south = inner([pltpu.roll(m[0:rows], 1, 1) for m in mid])
        above, below = inner(plane(second_ref, up)), inner(plane(second_ref, down))
        new = sweep(inner(mid), east, west, north, south, above, below)
        for c in range(3):
            last_ref[c, z] = new[c]
        return carry

    def store(n):
        span = pl.ds(n * chunk, chunk)
        return pltpu.make_async_copy(
            last_ref.at[:, span], fluid_ref.at[:, span], out_sem.at[n])

    slots = jnp.concatenate([table_ref[:, 0, :][:, p:p + 1] for p in range(per_owner)], axis=0)
    cells = chunk * rows
    for n in range(chunks):
        lax.fori_loop(n * chunk, (n + 1) * chunk, step_two, 0)
        store(n).start()
        taking = (iota((total, cells), 1) + n * cells == slots).astype(F32).astype(BF16)
        for c in range(3):
            flat = last_ref[c, n * chunk:(n + 1) * chunk].reshape(cells, columns).astype(BF16)
            part = jnp.dot(taking, flat, preferred_element_type=F32)
            sum_ref[c] = part if n == 0 else sum_ref[c] + part
    width = 3 * tiles * per_owner
    for c in range(3):
        for p in range(per_owner):
            for t in range(tiles):
                stage_ref[pl.ds(p * 3 * tiles + c * tiles + t, devices, stride=width), :] = (
                    sum_ref[c, p * devices:(p + 1) * devices, t * LANES:(t + 1) * LANES]
                )
    replies_ref[...] = stage_ref[...].reshape(replies_ref.shape).astype(BF16)
    for n in range(chunks):
        store(n).wait()


def gather_kernel(
    devices, per_owner, returned_ref, owners_ref, points_ref, weights_ref,
    out_ref, stage_ref, picked_ref,
):
    b = pl.program_id(0)
    k, points, patch = weights_ref.shape[1:]
    tiles = patch // LANES
    total = devices * per_owner

    @pl.when(b == 0)
    def _():
        stage_ref[...] = returned_ref[...].astype(F32).reshape(stage_ref.shape)
        owner_row = owners_ref[...]
        owner_column = to_column(owner_row)
        places = slot_column(owner_row, owner_column, devices)
        selector = (iota((places.shape[0], total), 1) == places).astype(F32).astype(BF16)
        for c in range(3):
            replies = unpack(stage_ref, devices, per_owner, tiles, c).astype(BF16)
            picked_ref[c] = jnp.dot(selector, replies, preferred_element_type=F32)

    span = pl.ds(pl.multiple_of(b * k, k), k)
    rows = [picked_ref[c, span, :] for c in range(3)]
    rows.append(jnp.zeros_like(rows[0]))
    left = jnp.concatenate(rows, axis=0).astype(BF16)
    right = weights_ref[0].reshape(k * points, patch)
    result = lax.dot_general(
        left, right, (((1,), (1,)), ((), ())), preferred_element_type=F32)
    diagonal = iota((k, k * points), 0) == iota((k, k * points), 1) // points
    for c in range(3):
        own = jnp.where(diagonal, result[c * k:(c + 1) * k], 0.0)
        fold = own[:, 0:points]
        for n in range(1, k):
            fold = fold + own[:, n * points:(n + 1) * points]
        interp = jnp.sum(fold, axis=0, keepdims=True)
        out_ref[0, c:c + 1, :] = points_ref[0, c:c + 1, :] + fiber_step * interp


def shards(rows_grid, columns_grid, velocity, fiber_points, stiffness, links, delta_weights,
           owners, patch_slots):
    blocks, intersection, points, patch = delta_weights.shape
    _, layers, rows, columns = velocity.shape
    devices = rows_grid * columns_grid
    entries = blocks * intersection
    per_owner = max(2, (2 * entries + devices - 1) // devices)
    total = devices * per_owner
    tiles = patch // LANES
    width = 3 * tiles * per_owner
    owner_row = owners.reshape(1, entries)
    slots_row = patch_slots.reshape(1, entries)
    whole = lambda shape: pl.BlockSpec(shape, lambda i: (0,) * len(shape))
    weight_spec = pl.BlockSpec((1, intersection, points, patch), lambda b: (b, 0, 0, 0))

    message = jax.ShapeDtypeStruct((devices, width, LANES), BF16)
    table_shape = jax.ShapeDtypeStruct((devices, 1, LANES), I32)
    stage = pltpu.VMEM((devices * width, LANES), F32)
    outgoing, table = pl.pallas_call(
        functools.partial(spread_kernel, devices, per_owner),
        grid=(blocks,),
        out_shape=[message, table_shape],
        in_specs=[
            whole(fiber_points.shape), whole((blocks, 1)), whole(links.shape),
            whole((1, entries)), whole((1, entries)), weight_spec,
        ],
        out_specs=[whole(message.shape), whole(table_shape.shape)],
        scratch_shapes=[
            pltpu.VMEM((3, blocks, points), F32), pltpu.VMEM((3, entries, patch), F32), stage,
        ],
    )(fiber_points, stiffness.reshape(blocks, 1), links, owner_row, slots_row, delta_weights)

    received, slots = swap([outgoing, table], rows_grid, columns_grid, 0)

    depth = 8
    sides_shape = (2, 3, 2, layers, columns)
    u, sides, ends, corners = pl.pallas_call(
        functools.partial(add_kernel, devices, per_owner),
        grid=(layers // depth,),
        out_shape=[
            jax.ShapeDtypeStruct(velocity.shape, F32),
            jax.ShapeDtypeStruct(sides_shape, BF16),
            jax.ShapeDtypeStruct((3, 16, layers * rows), BF16),
            jax.ShapeDtypeStruct((3, 16, LANES), BF16),
        ],
        in_specs=[
            whole(message.shape), whole(table_shape.shape),
            pl.BlockSpec((3, depth, rows, columns), lambda i: (0, i, 0, 0)),
        ],
        out_specs=[
            pl.BlockSpec((3, depth, rows, columns), lambda i: (0, i, 0, 0)),
            whole(sides_shape),
            pl.BlockSpec((3, 16, depth * rows), lambda i: (0, 0, i)),
            whole((3, 16, LANES)),
        ],
        scratch_shapes=[
            stage, pltpu.VMEM((3, total, patch), BF16), pltpu.VMEM(sides_shape, F32),
            pltpu.VMEM((3, 16, LANES), F32),
        ],
    )(received, slots, velocity)

    sides, ends, corners = pl.pallas_call(
        functools.partial(halo_kernel, rows_grid, columns_grid),
        out_shape=[
            jax.ShapeDtypeStruct(sides.shape, BF16),
            jax.ShapeDtypeStruct((2,) + ends.shape, BF16),
            jax.ShapeDtypeStruct((4,) + corners.shape, BF16),
        ],
        in_specs=[VMEM] * 3,
        out_specs=[VMEM] * 3,
        scratch_shapes=[pltpu.SemaphoreType.DMA((8,)), pltpu.SemaphoreType.DMA((8,))],
        compiler_params=pltpu.CompilerParams(collective_id=1, has_side_effects=True),
    )(sides, ends, corners)

    gx, gy = lax.axis_index("gx"), lax.axis_index("gy")
    flags = jnp.stack([gx > 0, gx < rows_grid - 1, gy > 0, gy < columns_grid - 1]).astype(I32)
    chunk = depth
    extended = (3, layers, rows + 8, columns + LANES)
    fluid, replies = pl.pallas_call(
        functools.partial(sweeps_kernel, devices, per_owner, chunk),
        out_shape=[jax.ShapeDtypeStruct(velocity.shape, F32), message],
        in_specs=[SMEM, VMEM, VMEM, VMEM, VMEM, ANY],
        out_specs=[ANY, VMEM],
        scratch_shapes=[
            pltpu.VMEM(extended, F32), pltpu.VMEM(extended, F32), pltpu.VMEM(velocity.shape, F32),
            pltpu.VMEM((2, 3, 2, layers, columns + LANES), F32), stage,
            pltpu.VMEM((3, total, patch), F32),
            pltpu.SemaphoreType.DMA((layers // chunk,)),
            pltpu.SemaphoreType.DMA((layers // chunk,)),
        ],
    )(flags, sides, ends, corners, slots, u)

    (returned,) = swap([replies], rows_grid, columns_grid, 2)

    moved = pl.pallas_call(
        functools.partial(gather_kernel, devices, per_owner),
        grid=(blocks,),
        out_shape=jax.ShapeDtypeStruct(fiber_points.shape, F32),
        in_specs=[
            whole(message.shape), whole((1, entries)),
            pl.BlockSpec((1, 3, points), lambda b: (b, 0, 0)), weight_spec,
        ],
        out_specs=pl.BlockSpec((1, 3, points), lambda b: (b, 0, 0)),
        scratch_shapes=[stage, pltpu.VMEM((3, entries, patch), F32)],
    )(returned, owner_row, fiber_points, delta_weights)
    return fluid, moved


def solution(mesh):
    placed = (
        P(None, None, "gx", "gy"),
        P(("gx", "gy"), None, None),
        P(("gx", "gy")),
        P(("gx", "gy"), None),
        P(("gx", "gy"), None, None, None),
        P(("gx", "gy"), None, None),
        P(("gx", "gy"), None),
    )
    return jax.shard_map(
        functools.partial(shards, mesh.shape["gx"], mesh.shape["gy"]),
        mesh=mesh,
        in_specs=placed,
        out_specs=(placed[0], placed[1]),
        check_vma=False,
    )
```

time: 220 us -> 111 us (0.50)
  Pallas kernels: 0 us -> 101 us
  local copies, waits for them, and re-layouts: 66.4 us -> 6.45 us
  other arithmetic: 59.4 us -> 1.96 us
  starting transfers between devices: 31.8 us -> 0 us
  waiting for transfers between devices: 25 us -> 0 us
  blocking collectives: 18.6 us -> 0 us
  matrix products: 16.5 us -> 0 us
    pallas_call x0 -> x7, Pallas kernels: none -> 101 us  [the longest x2 35.5 us: swap(): pl.pallas_call(functools.partial(swap_kernel, rows, columns, count), out_...]
    sub x1 -> x0, other arithmetic: 23.8 us -> none  [advance(): return middle + viscosity * laplace - transport_rate * transport]
    slice x10 -> x0, local copies, waits for them, and re-layouts: 23.6 us -> none  [the longest x4 14.9 us: advance(): above_cells = jnp.roll(middle, -1, axis=1)]
    convert_element_type x1, other arithmetic: 21.3 us -> 0.61 us  [shards(): jnp.stack([gx > 0, gx < rows_grid - 1, gy > 0, gy < columns_grid - 1])]
    all_to_all x2 -> x0, waiting for transfers between devices: 18.7 us -> none  [the longest x1 18.7 us: shards(): lax.all_to_all(outgoing.reshape(device_count, per_owner, 3, patch), ('gx'...]
    ppermute x8 -> x0, starting transfers between devices: 18.7 us -> none  [the longest x4 13.3 us: extended_2(): lax.ppermute(tail, axis, [(i, (i + 1) % count) for i in range(ends)])]
    all_to_all x1 -> x0, blocking collectives: 18.6 us -> none  [shards(): lax.all_to_all(replies.reshape(device_count, per_owner, 3, patch), ('gx',...]
    gather x3 -> x0, local copies, waits for them, and re-layouts: 18.5 us -> none  [shards(): partner_points = jnp.take_along_axis(fiber_points, partner_full, axis=2)]
  transfers between devices with their start and end apart: 10 -> 0, of which waited for: 3 -> 0; matrix products, arithmetic and copies ran while one was open for 17% -> 0% of each run, Pallas kernels for 0% -> 0%
where the time goes in v1:
time: 111 us; the launch traced here: 110 us
  Pallas kernels  101 us (91%)
  local copies, waits for them, and re-layouts  6.45 us (6%)
  other arithmetic  1.96 us (2%)
    pallas_call x2, Pallas kernels, swap(): pl.pallas_call(functools.partial(swap_kernel, rows, columns, count), out_...  35.5 us
    pallas_call x1, Pallas kernels, shards(): pl.pallas_call(functools.partial(sweeps_kernel, devices, per_owner, chunk...  26.1 us
    pallas_call x1, Pallas kernels, shards(): pl.pallas_call(functools.partial(halo_kernel, rows_grid, columns_grid), o...  13.5 us
    pallas_call x1, Pallas kernels, shards(): pl.pallas_call(functools.partial(add_kernel, devices, per_owner), grid=(l...  9.54 us
    pallas_call x1, Pallas kernels, shards(): pl.pallas_call(functools.partial(gather_kernel, devices, per_owner), grid...  8.62 us
    pallas_call x1, Pallas kernels, shards(): pl.pallas_call(functools.partial(spread_kernel, devices, per_owner), grid...  7.94 us
    unnamed x3, local copies, waits for them, and re-layouts  3.13 us

profile of v1, /device:TPU:0, one launch (start us, length us, event | category | flops | bytes accessed | tf_op | source)
XLA Modules:
  0.0 110.3 jit_solution(1097676703229677034)
XLA Ops:
  0.6 0.6 add_convert_fusion.flags_ref
  1.3 1.3 %reshape.15.slots_ref = s32[1,64]{1,0:T(1,128)} reshape(s32[8,8]{1,0:T(8,128)} %param.13) | data formatting | bytes 512 | tf_op jit(solution)/shard_map/reshape | solution.py:449
  2.6 0.5 broadcast.3
  3.1 1.3 %reduce.3 = s32[8,8]{1,0:T(8,128)S(1)} reduce(s32[8,8,1]{1,2,0:T(1,128)} %param.12, s32[]{:T(128)} %broadcast.3), dimensions={2}, to_apply=%param.12.reduce_sub_computation.3 | reduce | bytes 516 | tf_op args[5]
  4.5 0.7 reshape.14.owners_ref
  5.1 1.3 %copy.10.stiffness_ref = f32[8,1]{1,0:T(8,128)} copy(f32[8,1]{0,1:T(1,128)} %bitcast.6) | data formatting | bytes 64 | tf_op jit(solution)/shard_map/reshape | solution.py:468
  6.4 1.3 %copy.9.points_ref = f32[8,3,128]{2,1,0:T(4,128)} copy(f32[8,3,128]{2,0,1:T(8,128)} %param.8) | data formatting | bytes 24576 | tf_op args[1]
  7.7 7.9 %shard_map.86 = (bf16[32,48,128]{2,1,0:T(8,128)(2,1)}, s32[32,1,128]{2,1,0:T(1,128)}) custom-call(f32[8,3,128]{2,1,0:T(4,128)} %copy.9.points_ref, f32[8,1]{1,0:T(8,128)} %copy.10.stiffness_ref, s32[8,128]{1,0:T(8,128)} %links_ref.1, s32[1,64]{1,0:T(1,128)} %reshape.14.owners_ref, s32[1,64]{1,0:T(1,128)} %reshape.15.slots_ref, ...), custom_call_target="tpu_custom_call" | custom-call | tf_op jit(solution)/shard_map/pallas_call | solution.py:456
  15.7 20.1 %shard_map.87 = (bf16[32,48,128]{2,1,0:T(8,128)(2,1)}, s32[32,1,128]{2,1,0:T(1,128)}) custom-call(bf16[32,48,128]{2,1,0:T(8,128)(2,1)} %get-tuple-element.15.refs_0_, s32[32,1,128]{2,1,0:T(1,128)} %get-tuple-element.16.refs_1_), custom_call_target="tpu_custom_call" | custom-call | tf_op jit(solution)/shard_map/pallas_call | solution.py:159
  35.8 9.5 %shard_map.88 = (f32[3,32,32,512]{3,2,1,0:T(8,128)}, bf16[2,3,2,32,512]{4,3,2,1,0:T(8,128)(2,1)}, bf16[3,16,1024]{2,1,0:T(8,128)(2,1)}, bf16[3,16,128]{2,1,0:T(8,128)(2,1)}) custom-call(bf16[32,48,128]{2,1,0:T(8,128)(2,1)} %get-tuple-element.17.received_ref, s32[32,1,128]{2,1,0:T(1,128)} %get-tuple-element.18.table_ref, f32[3,32,32,512]{3,2,1,0:T(8,128)} %velocity_ref.1), custom_call_target="tpu_custom_call" | custom-call | tf_op jit(solution)/shard_map/pallas_call | solution.py:474
  45.4 13.5 %shard_map.89 = (bf16[2,3,2,32,512]{4,3,2,1,0:T(8,128)(2,1)}, bf16[2,3,16,1024]{3,2,1,0:T(8,128)(2,1)}, bf16[4,3,16,128]{3,2,1,0:T(8,128)(2,1)}) custom-call(bf16[2,3,2,32,512]{4,3,2,1,0:T(8,128)(2,1)} %get-tuple-element.19.sides_ref, bf16[3,16,1024]{2,1,0:T(8,128)(2,1)} %get-tuple-element.20.ends_ref, bf16[3,16,128]{2,1,0:T(8,128)(2,1)} %get-tuple-element.21.corners_ref), custom_call_target="tpu_custom_call" | custom-call | tf_op jit(solution)/shard_map/pallas_call | solution.py:499
  58.9 26.1 %shard_map.90 = (f32[3,32,32,512]{3,2,1,0:T(8,128)}, bf16[32,48,128]{2,1,0:T(8,128)(2,1)}) custom-call(s32[4]{0:T(128)} %add_convert_fusion.flags_ref, bf16[2,3,2,32,512]{4,3,2,1,0:T(8,128)(2,1)} %get-tuple-element.22.sides_ref, bf16[2,3,16,1024]{3,2,1,0:T(8,128)(2,1)} %get-tuple-element.23.ends_ref, bf16[4,3,16,128]{3,2,1,0:T(8,128)(2,1)} %get-tuple-element.24.corners_ref, ...), custom_call_target="tpu_custom_call" | custom-call | tf_op jit(solution)/shard_map/pallas_call | solution.py:516
  85.0 15.3 %shard_map.91.returned_ref = bf16[32,48,128]{2,1,0:T(8,128)(2,1)} custom-call(bf16[32,48,128]{2,1,0:T(8,128)(2,1)} %get-tuple-element.27.refs_0_), custom_call_target="tpu_custom_call" | custom-call | tf_op jit(solution)/shard_map/pallas_call | solution.py:159
  100.3 8.6 %shard_map.92 = f32[8,3,128]{2,1,0:T(4,128)} custom-call(bf16[32,48,128]{2,1,0:T(8,128)(2,1)} %shard_map.91.returned_ref, s32[1,64]{1,0:T(1,128)} %reshape.14.owners_ref, f32[8,3,128]{2,1,0:T(4,128)} %copy.9.points_ref, bf16[8,8,128,512]{3,2,1,0:T(8,128)(2,1)} %weights_ref.3), custom_call_target="tpu_custom_call" | custom-call | tf_op jit(solution)/shard_map/pallas_call | solution.py:532
  109.0 1.3 %copy.12 = f32[8,3,128]{2,0,1:T(8,128)} copy(f32[8,3,128]{2,1,0:T(4,128)} %shard_map.92) | data formatting | bytes 24576

commit v2 on v1

v2 whole, which is shorter than its diff:
```python
import functools

import jax
import jax.numpy as jnp
from jax import lax
from jax.experimental import pallas as pl
from jax.experimental.pallas import tpu as pltpu
from jax.sharding import PartitionSpec as P

STEPS = 2
viscosity = 0.1
transport_rate = 0.1
force_step = 0.5
fiber_step = 0.25

F32 = jnp.float32
BF16 = jnp.bfloat16
I32 = jnp.int32
LANES = 128
MESH = pl.DeviceIdType.MESH
VMEM = pl.BlockSpec(memory_space=pltpu.VMEM)
ANY = pl.BlockSpec(memory_space=pl.ANY)
SMEM = pl.BlockSpec(memory_space=pltpu.SMEM)


def iota(shape, dim):
    return lax.broadcasted_iota(I32, shape, dim)


def to_column(row):
    n = row.shape[1]
    return jnp.sum(jnp.where(iota((n, n), 0) == iota((n, n), 1), row, 0), axis=1, keepdims=True)


def to_row(grid):
    n, k = grid.shape
    tiled = jnp.concatenate([grid] * n, axis=1)
    return jnp.sum(
        jnp.where(iota((n, n * k), 0) == iota((n, n * k), 1) // k, tiled, 0), axis=0, keepdims=True)


def slot_row(owner_row, owner_column, devices):
    n = owner_row.shape[1]
    same = (owner_column == owner_row) & (iota((n, n), 0) < iota((n, n), 1))
    rank = jnp.sum(jnp.where(same, 1, 0), axis=0, keepdims=True)
    return rank * devices + owner_row


def slot_column(owner_row, owner_column, devices):
    n = owner_row.shape[1]
    same = (owner_column == owner_row) & (iota((n, n), 1) < iota((n, n), 0))
    rank = jnp.sum(jnp.where(same, 1, 0), axis=1, keepdims=True)
    return rank * devices + owner_column


def spread_kernel(
    devices, per_owner, points_ref, stiffness_ref, links_ref, owners_ref, slots_ref, weights_ref,
    out_ref, table_ref, force_ref, contrib_ref, stage_ref,
):
    b = pl.program_id(0)
    blocks = pl.num_programs(0)
    k, points, patch = weights_ref.shape[1:]

    @pl.when(b == 0)
    def _():
        partner = lax.rem(iota(links_ref.shape, 1) + links_ref[...], points)
        for c in range(3):
            here = points_ref[c]
            there = jnp.take_along_axis(here, partner, axis=1)
            force_ref[c] = there - here

    diagonal = iota((k, k * points), 0) == iota((k, k * points), 1) // points
    rows = []
    for c in range(3):
        row = stiffness_ref[b] * force_ref[c, pl.ds(b, 1), :]
        rows.append(jnp.where(diagonal, jnp.concatenate([row] * k, axis=1), 0.0))
    rows.append(jnp.zeros_like(rows[0]))
    left = jnp.concatenate(rows, axis=0).astype(BF16)
    right = weights_ref[0].reshape(k * points, patch)
    result = jnp.dot(left, right, preferred_element_type=F32)
    for c in range(3):
        contrib_ref[c, pl.ds(pl.multiple_of(b * k, k), k), :] = result[c * k:(c + 1) * k]

    @pl.when(b == blocks - 1)
    def _():
        owner_row = to_row(owners_ref[:, 0, :])
        owner_column = to_column(owner_row)
        places = slot_row(owner_row, owner_column, devices)
        total = devices * per_owner
        chosen = iota((total, places.shape[1]), 0) == places
        selector = chosen.astype(F32).astype(BF16)
        tiles = patch // LANES
        width = 3 * tiles * per_owner
        for c in range(3):
            packed = jnp.dot(selector, contrib_ref[c].astype(BF16), preferred_element_type=F32)
            for p in range(per_owner):
                for t in range(tiles):
                    stage_ref[pl.ds(p * 3 * tiles + c * tiles + t, devices, stride=width), :] = (
                        packed[p * devices:(p + 1) * devices, t * LANES:(t + 1) * LANES]
                    )
        out_ref[...] = stage_ref[...].reshape(out_ref.shape).astype(BF16)
        column = jnp.max(jnp.where(chosen, to_row(slots_ref[...]), -1), axis=1, keepdims=True)
        lane = iota((devices, LANES), 1)
        table = jnp.full((devices, LANES), -1, I32)
        for p in range(per_owner):
            table = jnp.where(lane == p, column[p * devices:(p + 1) * devices], table)
        for d in range(devices):
            table_ref[d] = table[d:d + 1]


def start_swap(rows, columns, ins, outs, send_sem, recv_sem, own_sem):
    devices = rows * columns
    count = len(ins)
    me = lax.axis_index("gx") * columns + lax.axis_index("gy")

    def place(d):
        return (d // columns, lax.rem(d, columns))

    barrier = pltpu.get_barrier_semaphore()

    def hello(off, carry):
        other = lax.rem(me + off, devices)
        pl.semaphore_signal(barrier, inc=1, device_id=place(other), device_id_type=MESH)
        return carry

    lax.fori_loop(1, devices, hello, 0)
    pl.semaphore_wait(barrier, devices - 1)

    def copy(n, off):
        other = lax.rem(me + off, devices)
        return pltpu.make_async_remote_copy(
            src_ref=ins[n].at[other], dst_ref=outs[n].at[me],
            send_sem=send_sem.at[n, off], recv_sem=recv_sem.at[n, off],
            device_id=place(other), device_id_type=MESH,
        )

    def start(off, carry):
        for n in range(count):
            copy(n, off).start()
        return carry

    def finish(off, carry):
        for n in range(count):
            copy(n, off).wait()
        return carry

    def own(n):
        return pltpu.make_async_copy(ins[n].at[me], outs[n].at[me], own_sem.at[n])

    lax.fori_loop(1, devices, start, 0)
    for n in range(count):
        own(n).start()

    def wait():
        for n in range(count):
            own(n).wait()
        lax.fori_loop(1, devices, finish, 0)

    return wait


def swap_sems(count, devices):
    return [
        pltpu.SemaphoreType.DMA((count, devices)),
        pltpu.SemaphoreType.DMA((count, devices)),
        pltpu.SemaphoreType.DMA((count,)),
    ]


def unpack(stage_ref, devices, per_owner, tiles, c):
    width = 3 * tiles * per_owner
    rows = []
    for p in range(per_owner):
        rows.append(jnp.concatenate(
            [stage_ref[pl.ds(p * 3 * tiles + c * tiles + t, devices, stride=width), :]
             for t in range(tiles)], axis=1))
    return jnp.concatenate(rows, axis=0)


def table_row(table_ref, devices, per_owner):
    total = devices * per_owner
    row = jnp.zeros((1, total), I32)
    for p in range(per_owner):
        column = table_ref[:, 0, :][:, p:p + 1]
        spot = iota((devices, total), 1) == p * devices + iota((devices, total), 0)
        row = row + jnp.sum(jnp.where(spot, column, 0), axis=0, keepdims=True)
    return row


def table_column(table_ref, per_owner):
    return jnp.concatenate([table_ref[:, 0, :][:, p:p + 1] for p in range(per_owner)], axis=0)


def one_hot(mask):
    return mask.astype(F32).astype(BF16)


def dispatch_kernel(
    rows_grid, columns_grid, per_owner, out_ref, outtable_ref, velocity_ref,
    received_ref, table_ref, sides_out, ends_out, corners_out,
    row_ref, end_ref, edge_ref, ends_ref, stage_ref, force_ref, sides_send, ends_send,
    corners_send, send_sem, recv_sem, own_sem, load_sem, hsend_sem, hrecv_sem,
):
    devices = rows_grid * columns_grid
    total = devices * per_owner
    _, layers, rows, columns = velocity_ref.shape
    tiles = columns // LANES
    cells = layers * rows
    loads = []
    for side in range(2):
        loads.append(pltpu.make_async_copy(
            velocity_ref.at[:, :, pl.ds(side * (rows - 8), 8), :], row_ref.at[side],
            load_sem.at[side]))
        loads.append(pltpu.make_async_copy(
            velocity_ref.at[:, :, :, pl.ds(side * (columns - LANES), LANES)], end_ref.at[side],
            load_sem.at[2 + side]))
    for load in loads:
        load.start()
    wait = start_swap(
        rows_grid, columns_grid, [out_ref, outtable_ref], [received_ref, table_ref],
        send_sem, recv_sem, own_sem)

    cell, want = iota((cells, LANES), 0), iota((cells, LANES), 1)
    z, x = cell // rows, lax.rem(cell, rows)
    edge_ref[...] = one_hot((x == 0) & (want == z) | (x == rows - 1) & (want == layers + z))
    r8, l8 = iota((8, LANES), 0), iota((8, LANES), 1)

    def pick(side, c):
        r = r8 - 2 * c
        return one_hot((r >= 0) & (r < 2) & (l8 == r + side * (LANES - 2)))

    for load in loads:
        load.wait()
    across = (((1,), (1,)), ((), ()))
    for side in range(2):
        found = jnp.zeros((8, cells), F32)
        for c in range(3):
            flat = end_ref[side, c].reshape(cells, LANES)
            high = flat.astype(BF16)
            low = (flat - high.astype(F32)).astype(BF16)
            for part in (high, low):
                found = found + lax.dot_general(
                    pick(side, c), part, across, preferred_element_type=F32)
        ends_ref[side] = found

    wait()

    stage_ref[...] = received_ref[...].astype(F32).reshape(stage_ref.shape)
    slots_row = table_row(table_ref, devices, per_owner)
    slots_column = table_column(table_ref, per_owner)
    e = iota((4 * layers, total), 0)
    line, z = e // layers, lax.rem(e, layers)
    x = jnp.where(line < 2, line, rows - 4 + line)
    placing = one_hot(z * rows + x == slots_row)
    for c in range(3):
        force = unpack(stage_ref, devices, per_owner, tiles, c).astype(BF16)
        force_ref[c] = force
        push = jnp.dot(placing, force, preferred_element_type=F32)
        for side in range(2):
            for r in range(2):
                n = side * 2 + r
                v = row_ref[side, c, :, 6 * side + r, :]
                v = v + force_step * push[n * layers:(n + 1) * layers]
                sides_send[side, c, r] = v.astype(BF16)

    gx, gy = lax.axis_index("gx"), lax.axis_index("gy")
    west, east, south, north = gx > 0, gx < rows_grid - 1, gy > 0, gy < columns_grid - 1
    plan = [
        (sides_send.at[0], sides_out.at[1], (-1, 0), west, east),
        (sides_send.at[1], sides_out.at[0], (1, 0), east, west),
        (ends_send.at[0], ends_out.at[1], (0, -1), south, north),
        (ends_send.at[1], ends_out.at[0], (0, 1), north, south),
        (corners_send.at[0], corners_out.at[3], (-1, -1), west & south, east & north),
        (corners_send.at[1], corners_out.at[2], (-1, 1), west & north, east & south),
        (corners_send.at[0], corners_out.at[1], (1, -1), east & south, west & north),
        (corners_send.at[1], corners_out.at[0], (1, 1), east & north, west & south),
    ]
    copies = []
    for n, (source, target, (dx, dy), _, _) in enumerate(plan):
        to = (lax.rem(gx + dx + rows_grid, rows_grid), lax.rem(gy + dy + columns_grid, columns_grid))
        copies.append(pltpu.make_async_remote_copy(
            src_ref=source, dst_ref=target, send_sem=hsend_sem.at[n], recv_sem=hrecv_sem.at[n],
            device_id=to, device_id_type=MESH))

    def go(n):
        @pl.when(plan[n][3])
        def _():
            copies[n].start()

    go(0)
    go(1)
    taking = one_hot(iota((total, cells), 1) == slots_column)
    for side in range(2):
        first = side * (columns - LANES)
        mine = jnp.zeros((8, total), F32)
        for c in range(3):
            mine = mine + lax.dot_general(
                pick(side, c), force_ref[c, :, first:first + LANES], across,
                preferred_element_type=F32)
        push = jnp.dot(mine.astype(BF16), taking, preferred_element_type=F32)
        ends = (ends_ref[side] + force_step * push).astype(BF16)
        ends_send[side] = ends
        corners_send[side] = jnp.dot(
            ends, edge_ref[...], preferred_element_type=F32).astype(BF16)
    for n in range(2, 8):
        go(n)
    for n in range(8):
        @pl.when(plan[n][3])
        def _():
            copies[n].wait_send()

        @pl.when(plan[n][4])
        def _():
            copies[n].wait_recv()


def sweep(mid, east, west, north, south, above, below):
    r = transport_rate
    coefficients = [(viscosity - r * m, viscosity + r * m) for m in mid]
    keep = 1.0 - 6.0 * viscosity
    out = []
    for c in range(3):
        v = keep * mid[c]
        for (ahead, behind), (front, back) in zip(
            coefficients, ((east, west), (north, south), (above, below))
        ):
            v = v + (ahead * front[c] + behind * back[c])
        out.append(v)
    return out


def sweeps_kernel(
    devices, per_owner, rows_grid, columns_grid, chunk, sides_ref, ends_ref, corners_ref,
    table_ref, received_ref, velocity_ref,
    fluid_ref, replies_ref, first_ref, second_ref, last_ref, side_ref, stage_ref, sum_ref,
    force_ref, in_sem, out_sem,
):
    _, layers, rows, columns = velocity_ref.shape
    tiles = columns // LANES
    total = devices * per_owner
    chunks = layers // chunk
    cells = chunk * rows
    tall, wide = rows + 8, columns + LANES

    def load(n):
        span = pl.ds(n * chunk, chunk)
        return pltpu.make_async_copy(
            velocity_ref.at[:, span], first_ref.at[:, span, 0:rows, 0:columns], in_sem.at[n])

    for n in range(chunks):
        load(n).start()

    gx, gy = lax.axis_index("gx"), lax.axis_index("gy")
    has = [gx > 0, gx < rows_grid - 1, gy > 0, gy < columns_grid - 1]
    for side in range(2):
        side_ref[side, :, :, :, 0:columns] = jnp.where(has[side], sides_ref[side].astype(F32), 0.0)
        side_ref[side, :, :, :, columns:] = jnp.zeros((3, 2, layers, LANES), F32)
    r8, l8 = iota((8, LANES), 0), iota((8, LANES), 1)

    def expand(ref, n, side, c, there):
        r = r8 - 2 * c
        pick = one_hot((r >= 0) & (r < 2) & (l8 == r + (1 - side) * (LANES - 2)))
        values = jnp.where(there, ref[n].astype(F32), 0.0).astype(BF16)
        return lax.dot_general(
            values, pick, (((0,), (0,)), ((), ())), preferred_element_type=F32)

    for c in range(3):
        band = expand(ends_ref, 0, 0, c, has[2]) + expand(ends_ref, 1, 1, c, has[3])
        first_ref[c, :, 0:rows, columns:] = band.reshape(layers, rows, LANES)
        low = expand(corners_ref, 0, 0, c, has[0] & has[2])
        low = low + expand(corners_ref, 1, 1, c, has[0] & has[3])
        high = expand(corners_ref, 2, 0, c, has[1] & has[2])
        high = high + expand(corners_ref, 3, 1, c, has[1] & has[3])
        side_ref[0, c, 1, :, columns:] = low[layers:2 * layers]
        side_ref[1, c, 0, :, columns:] = high[0:layers]

    wide8 = iota((8, wide), 0)

    def border(z, carry):
        for c in range(3):
            tile = jnp.zeros((8, wide), F32)
            for place, side, r in ((0, 1, 0), (1, 1, 1), (6, 0, 0), (7, 0, 1)):
                tile = jnp.where(wide8 == place, side_ref[side, c, r, pl.ds(z, 1), :], tile)
            first_ref[c, pl.ds(z, 1), rows:, :] = tile[None]
        return carry

    lax.fori_loop(0, layers, border, 0)

    stage_ref[...] = received_ref[...].astype(F32).reshape(stage_ref.shape)
    for c in range(3):
        force_ref[c] = (force_step * unpack(stage_ref, devices, per_owner, tiles, c)).astype(BF16)
    slots_row = table_row(table_ref, devices, per_owner)
    for n in range(chunks):
        load(n).wait()
        placing = one_hot(iota((cells, total), 0) + n * cells == slots_row)
        span = slice(n * chunk, (n + 1) * chunk)
        for c in range(3):
            push = jnp.dot(placing, force_ref[c], preferred_element_type=F32)
            first_ref[c, span, 0:rows, 0:columns] += push.reshape(chunk, rows, columns)

    lane8 = iota((8, wide), 1)
    lane_keep = (lane8 < columns) | (lane8 == columns) & has[3] | (lane8 == wide - 1) & has[2]
    row_keep = (wide8 == 0) & has[1] | (wide8 == 7) & has[0]

    def tile(ref, c, z, t, width):
        return ref[c, z, 8 * t:8 * t + 8, 0:width]

    def neighbours(ref, z, t, width):
        count = tall // 8
        up, down = lax.rem(z + 1, layers), lax.rem(z + layers - 1, layers)
        row = wide8[:, 0:width]
        out = []
        for c in range(3):
            full = tile(ref, c, z, t, wide)
            mid = full[:, 0:width]
            after = tile(ref, c, z, (t + 1) % count, width)
            before = tile(ref, c, z, (t + count - 1) % count, width)
            east = pltpu.roll(jnp.where(row == 0, after, mid), 7, 0)
            west = pltpu.roll(jnp.where(row == 7, before, mid), 1, 0)
            north = pltpu.roll(full, wide - 1, 1)[:, 0:width]
            south = pltpu.roll(full, 1, 1)[:, 0:width]
            out.append((
                mid, east, west, north, south, tile(ref, c, up, t, width),
                tile(ref, c, down, t, width)))
        return [list(v) for v in zip(*out)]

    def step_one(z, carry):
        for t in range(tall // 8):
            new = sweep(*neighbours(first_ref, z, t, wide))
            keep = lane_keep if t < rows // 8 else lane_keep & row_keep
            for c in range(3):
                second_ref[c, z, 8 * t:8 * t + 8, :] = jnp.where(keep, new[c], 0.0)
        return carry

    lax.fori_loop(0, layers, step_one, 0)

    def step_two(z, carry):
        for t in range(rows // 8):
            new = sweep(*neighbours(second_ref, z, t, columns))
            for c in range(3):
                last_ref[c, z, 8 * t:8 * t + 8, :] = new[c]
        return carry

    def store(n):
        span = pl.ds(n * chunk, chunk)
        return pltpu.make_async_copy(
            last_ref.at[:, span], fluid_ref.at[:, span], out_sem.at[n])

    slots = table_column(table_ref, per_owner)
    for n in range(chunks):
        lax.fori_loop(n * chunk, (n + 1) * chunk, step_two, 0)
        store(n).start()
        taking = one_hot(iota((total, cells), 1) + n * cells == slots)
        for c in range(3):
            flat = last_ref[c, n * chunk:(n + 1) * chunk].reshape(cells, columns).astype(BF16)
            part = jnp.dot(taking, flat, preferred_element_type=F32)
            sum_ref[c] = part if n == 0 else sum_ref[c] + part
    width = 3 * tiles * per_owner
    for c in range(3):
        for p in range(per_owner):
            for t in range(tiles):
                stage_ref[pl.ds(p * 3 * tiles + c * tiles + t, devices, stride=width), :] = (
                    sum_ref[c, p * devices:(p + 1) * devices, t * LANES:(t + 1) * LANES]
                )
    replies_ref[...] = stage_ref[...].reshape(replies_ref.shape).astype(BF16)
    for n in range(chunks):
        store(n).wait()


def gather_kernel(
    rows_grid, columns_grid, per_owner, replies_ref, owners_ref, points_ref, weights_ref,
    out_ref, returned_ref, loaded_ref, stage_ref, picked_ref, send_sem, recv_sem, own_sem, load_sem,
):
    devices = rows_grid * columns_grid
    blocks, k, points, patch = weights_ref.shape
    tiles = patch // LANES
    total = devices * per_owner

    def load(b):
        return pltpu.make_async_copy(weights_ref.at[b], loaded_ref.at[b], load_sem.at[b])

    for b in range(blocks):
        load(b).start()
    wait = start_swap(
        rows_grid, columns_grid, [replies_ref], [returned_ref], send_sem, recv_sem, own_sem)
    owner_row = to_row(owners_ref[:, 0, :])
    places = slot_column(owner_row, to_column(owner_row), devices)
    selector = one_hot(iota((places.shape[0], total), 1) == places)
    for b in range(blocks):
        load(b).wait()
    wait()
    stage_ref[...] = returned_ref[...].astype(F32).reshape(stage_ref.shape)
    for c in range(3):
        replies = unpack(stage_ref, devices, per_owner, tiles, c).astype(BF16)
        picked_ref[c] = jnp.dot(selector, replies, preferred_element_type=F32)
    diagonal = iota((k, k * points), 0) == iota((k, k * points), 1) // points
    for b in range(blocks):
        rows = [picked_ref[c, b * k:(b + 1) * k, :] for c in range(3)]
        rows.append(jnp.zeros_like(rows[0]))
        left = jnp.concatenate(rows, axis=0).astype(BF16)
        right = loaded_ref[b].reshape(k * points, patch)
        result = lax.dot_general(
            left, right, (((1,), (1,)), ((), ())), preferred_element_type=F32)
        for c in range(3):
            own = jnp.where(diagonal, result[c * k:(c + 1) * k], 0.0)
            fold = own[:, 0:points]
            for n in range(1, k):
                fold = fold + own[:, n * points:(n + 1) * points]
            interp = jnp.sum(fold, axis=0, keepdims=True)
            out_ref[c, b:b + 1, :] = points_ref[c, b:b + 1, :] + fiber_step * interp


def shards(rows_grid, columns_grid, velocity, fiber_points, stiffness, links, delta_weights,
           owners, patch_slots):
    blocks, intersection, points, patch = delta_weights.shape
    _, layers, rows, columns = velocity.shape
    devices = rows_grid * columns_grid
    entries = blocks * intersection
    per_owner = max(2, (2 * entries + devices - 1) // devices)
    total = devices * per_owner
    tiles = patch // LANES
    width = 3 * tiles * per_owner
    owners = jnp.transpose(owners, (0, 2, 1))
    points_first = jnp.transpose(fiber_points, (1, 0, 2))
    whole = lambda shape: pl.BlockSpec(shape, lambda i: (0,) * len(shape))
    message = jax.ShapeDtypeStruct((devices, width, LANES), BF16)
    table_shape = jax.ShapeDtypeStruct((devices, 1, LANES), I32)
    stage = pltpu.VMEM((devices * width, LANES), F32)
    outgoing, table = pl.pallas_call(
        functools.partial(spread_kernel, devices, per_owner),
        grid=(blocks,),
        out_shape=[message, table_shape],
        in_specs=[
            whole(points_first.shape), SMEM, whole(links.shape), whole(owners.shape),
            whole(patch_slots.shape),
            pl.BlockSpec((1, intersection, points, patch), lambda b: (b, 0, 0, 0)),
        ],
        out_specs=[whole(message.shape), whole(table_shape.shape)],
        scratch_shapes=[
            pltpu.VMEM((3, blocks, points), F32), pltpu.VMEM((3, entries, patch), F32), stage,
        ],
    )(points_first, stiffness, links, owners, patch_slots, delta_weights)

    sides_shape = (2, 3, 2, layers, columns)
    ends_shape = (2, 8, layers * rows)
    received, slots, sides, ends, corners = pl.pallas_call(
        functools.partial(dispatch_kernel, rows_grid, columns_grid, per_owner),
        out_shape=[
            message, table_shape,
            jax.ShapeDtypeStruct(sides_shape, BF16),
            jax.ShapeDtypeStruct(ends_shape, BF16),
            jax.ShapeDtypeStruct((4, 8, LANES), BF16),
        ],
        in_specs=[VMEM, VMEM, ANY],
        out_specs=[VMEM] * 5,
        scratch_shapes=[
            pltpu.VMEM((2, 3, layers, 8, columns), F32),
            pltpu.VMEM((2, 3, layers, rows, LANES), F32),
            pltpu.VMEM((layers * rows, LANES), BF16),
            pltpu.VMEM(ends_shape, F32),
            stage,
            pltpu.VMEM((3, total, patch), BF16),
            pltpu.VMEM(sides_shape, BF16),
            pltpu.VMEM(ends_shape, BF16),
            pltpu.VMEM((2, 8, LANES), BF16),
            *swap_sems(2, devices),
            pltpu.SemaphoreType.DMA((4,)),
            pltpu.SemaphoreType.DMA((8,)),
            pltpu.SemaphoreType.DMA((8,)),
        ],
        compiler_params=pltpu.CompilerParams(collective_id=0, has_side_effects=True),
    )(outgoing, table, velocity)

    chunk = 8
    extended = (3, layers, rows + 8, columns + LANES)
    fluid, replies = pl.pallas_call(
        functools.partial(sweeps_kernel, devices, per_owner, rows_grid, columns_grid, chunk),
        out_shape=[jax.ShapeDtypeStruct(velocity.shape, F32), message],
        in_specs=[VMEM] * 5 + [ANY],
        out_specs=[ANY, VMEM],
        scratch_shapes=[
            pltpu.VMEM(extended, F32), pltpu.VMEM(extended, F32), pltpu.VMEM(velocity.shape, F32),
            pltpu.VMEM((2, 3, 2, layers, columns + LANES), F32), stage,
            pltpu.VMEM((3, total, patch), F32), pltpu.VMEM((3, total, patch), BF16),
            pltpu.SemaphoreType.DMA((layers // chunk,)),
            pltpu.SemaphoreType.DMA((layers // chunk,)),
        ],
    )(sides, ends, corners, slots, received, velocity)

    moved = pl.pallas_call(
        functools.partial(gather_kernel, rows_grid, columns_grid, per_owner),
        out_shape=jax.ShapeDtypeStruct(points_first.shape, F32),
        in_specs=[VMEM, VMEM, VMEM, ANY],
        out_specs=VMEM,
        scratch_shapes=[
            pltpu.VMEM(message.shape, BF16), pltpu.VMEM(delta_weights.shape, BF16), stage,
            pltpu.VMEM((3, entries, patch), F32), *swap_sems(1, devices),
            pltpu.SemaphoreType.DMA((blocks,)),
        ],
        compiler_params=pltpu.CompilerParams(collective_id=1, has_side_effects=True),
    )(replies, owners, points_first, delta_weights)
    return fluid, jnp.transpose(moved, (1, 0, 2))


def solution(mesh):
    placed = (
        P(None, None, "gx", "gy"),
        P(("gx", "gy"), None, None),
        P(("gx", "gy")),
        P(("gx", "gy"), None),
        P(("gx", "gy"), None, None, None),
        P(("gx", "gy"), None, None),
        P(("gx", "gy"), None),
    )
    return jax.shard_map(
        functools.partial(shards, mesh.shape["gx"], mesh.shape["gy"]),
        mesh=mesh,
        in_specs=placed,
        out_specs=(placed[0], placed[1]),
        check_vma=False,
    )
```

time: 111 us -> 79.7 us (0.72)
  Pallas kernels: 101 us -> 77.4 us
  local copies, waits for them, and re-layouts: 6.45 us -> 1.31 us
  other arithmetic: 1.96 us -> 0 us
    pallas_call x6 -> x3, Pallas kernels: 93.2 us -> 69.3 us  [the longest x1 24.4 us: shards(): pl.pallas_call(functools.partial(dispatch_kernel, rows_grid, columns_grid...]
    reshape x3 -> x0, local copies, waits for them, and re-layouts: 3.32 us -> none  [the longest x1 1.34 us: shards(): slots_row = patch_slots.reshape(1, entries)]
    unnamed x3 -> x1, local copies, waits for them, and re-layouts: 3.13 us -> 1.31 us
    unnamed x1 -> x0, other arithmetic: 1.35 us -> none
where the time goes in v2:
time: 79.7 us; the launch traced here: 79.3 us
  Pallas kernels  77.4 us (97%)
  local copies, waits for them, and re-layouts  1.31 us (2%)
    pallas_call x1, Pallas kernels, shards(): pl.pallas_call(functools.partial(dispatch_kernel, rows_grid, columns_grid...  24.4 us
    pallas_call x1, Pallas kernels, shards(): pl.pallas_call(functools.partial(sweeps_kernel, devices, per_owner, rows_...  23.3 us
    pallas_call x1, Pallas kernels, shards(): pl.pallas_call(functools.partial(gather_kernel, rows_grid, columns_grid,...  21.6 us
    pallas_call x1, Pallas kernels, shards(): pl.pallas_call(functools.partial(spread_kernel, devices, per_owner), grid...  8.08 us

profile of v2, /device:TPU:0, one launch (start us, length us, event | category | flops | bytes accessed | tf_op | source)
XLA Modules:
  0.0 79.3 jit_solution(14248606881232243146)
XLA Ops:
  0.6 8.1 %shard_map.86 = (bf16[32,48,128]{2,1,0:T(8,128)(2,1)}, s32[32,1,128]{2,1,0:T(1,128)}) custom-call(f32[3,8,128]{2,1,0:T(8,128)} %bitcast.5, f32[8]{0:T(128)} %stiffness_ref.1, s32[8,128]{1,0:T(8,128)} %links_ref.1, s32[8,1,8]{2,1,0:T(1,128)} %bitcast.8, s32[8,8]{1,0:T(8,128)} %slots_ref.1, bf16[8,8,128,512]{3,2,1,0:T(8,128)(2,1)} %weights_ref.3), custom_call_target="tpu_custom_call" | custom-call | tf_op jit(solution)/shard_map/pallas_call | solution.py:529
  8.7 24.4 %shard_map.87 = (bf16[32,48,128]{2,1,0:T(8,128)(2,1)}, s32[32,1,128]{2,1,0:T(1,128)}, bf16[2,3,2,32,512]{4,3,2,1,0:T(8,128)(2,1)}, bf16[2,8,1024]{2,1,0:T(8,128)(2,1)}, bf16[4,8,128]{2,1,0:T(8,128)(2,1)}) custom-call(bf16[32,48,128]{2,1,0:T(8,128)(2,1)} %get-tuple-element.11.out_ref, s32[32,1,128]{2,1,0:T(1,128)} %get-tuple-element.12.outtable_ref, ...), custom_call_target="tpu_custom_call" | custom-call | tf_op jit(solution)/shard_map/pallas_call | solution.py:546
  33.1 23.3 %shard_map.88 = (f32[3,32,32,512]{3,2,1,0:T(8,128)}, bf16[32,48,128]{2,1,0:T(8,128)(2,1)}) custom-call(bf16[2,3,2,32,512]{4,3,2,1,0:T(8,128)(2,1)} %get-tuple-element.13.sides_ref, bf16[2,8,1024]{2,1,0:T(8,128)(2,1)} %get-tuple-element.14.ends_ref, bf16[4,8,128]{2,1,0:T(8,128)(2,1)} %get-tuple-element.15.corners_ref, ...), custom_call_target="tpu_custom_call" | custom-call | tf_op jit(solution)/shard_map/pallas_call | solution.py:576
  56.4 21.6 %shard_map.89 = f32[3,8,128]{2,1,0:T(8,128)} custom-call(bf16[32,48,128]{2,1,0:T(8,128)(2,1)} %get-tuple-element.19.replies_ref, s32[8,1,8]{2,1,0:T(1,128)} %bitcast.9, f32[3,8,128]{2,1,0:T(8,128)} %bitcast.6, bf16[8,8,128,512]{3,2,1,0:T(8,128)(2,1)} %weights_ref.3), custom_call_target="tpu_custom_call" | custom-call | tf_op jit(solution)/shard_map/pallas_call | solution.py:590
  78.0 1.3 %copy.12 = f32[8,3,128]{2,0,1:T(8,128)} copy(f32[8,3,128]{2,0,1:T(8,128)} %bitcast.7) | data formatting | bytes 24576

commit v3 on v2

--- a/solution.py
+++ b/solution.py
@@ -53,62 +53,69 @@
     return rank * devices + owner_column
 
 
-def spread_kernel(
-    devices, per_owner, points_ref, stiffness_ref, links_ref, owners_ref, slots_ref, weights_ref,
-    out_ref, table_ref, force_ref, contrib_ref, stage_ref,
+def spread(
+    devices, per_owner, points_ref, stiffness_ref, links_ref, owners_ref, slots_ref, loaded_ref,
+    out_ref, table_ref, contrib_ref, stage_ref, wait_block,
 ):
-    b = pl.program_id(0)
-    blocks = pl.num_programs(0)
-    k, points, patch = weights_ref.shape[1:]
-
-    @pl.when(b == 0)
-    def _():
-        partner = lax.rem(iota(links_ref.shape, 1) + links_ref[...], points)
-        for c in range(3):
-            here = points_ref[c]
-            there = jnp.take_along_axis(here, partner, axis=1)
-            force_ref[c] = there - here
-
+    blocks, k, points, patch = loaded_ref.shape
+    parts = []
+    for c in range(3):
+        rest = points_ref[c]
+        for _ in range(3):
+            part = rest.astype(BF16).astype(F32)
+            parts.append(part)
+            rest = rest - part
+    parts.append(jnp.zeros_like(parts[0]))
+    parts = jnp.concatenate(parts, axis=0).astype(BF16)
+    partner = lax.rem(iota(links_ref.shape, 1) + links_ref[...], points)
     diagonal = iota((k, k * points), 0) == iota((k, k * points), 1) // points
-    rows = []
-    for c in range(3):
-        row = stiffness_ref[b] * force_ref[c, pl.ds(b, 1), :]
-        rows.append(jnp.where(diagonal, jnp.concatenate([row] * k, axis=1), 0.0))
-    rows.append(jnp.zeros_like(rows[0]))
-    left = jnp.concatenate(rows, axis=0).astype(BF16)
-    right = weights_ref[0].reshape(k * points, patch)
-    result = jnp.dot(left, right, preferred_element_type=F32)
-    for c in range(3):
-        contrib_ref[c, pl.ds(pl.multiple_of(b * k, k), k), :] = result[c * k:(c + 1) * k]
-
-    @pl.when(b == blocks - 1)
-    def _():
-        owner_row = to_row(owners_ref[:, 0, :])
-        owner_column = to_column(owner_row)
-        places = slot_row(owner_row, owner_column, devices)
-        total = devices * per_owner
-        chosen = iota((total, places.shape[1]), 0) == places
-        selector = chosen.astype(F32).astype(BF16)
-        tiles = patch // LANES
-        width = 3 * tiles * per_owner
-        for c in range(3):
-            packed = jnp.dot(selector, contrib_ref[c].astype(BF16), preferred_element_type=F32)
-            for p in range(per_owner):
-                for t in range(tiles):
-                    stage_ref[pl.ds(p * 3 * tiles + c * tiles + t, devices, stride=width), :] = (
-                        packed[p * devices:(p + 1) * devices, t * LANES:(t + 1) * LANES]
-                    )
-        out_ref[...] = stage_ref[...].reshape(out_ref.shape).astype(BF16)
-        column = jnp.max(jnp.where(chosen, to_row(slots_ref[...]), -1), axis=1, keepdims=True)
-        lane = iota((devices, LANES), 1)
-        table = jnp.full((devices, LANES), -1, I32)
+    lefts = []
+    for b in range(blocks):
+        moving = one_hot(iota((points, points), 0) == partner[b:b + 1])
+        there = jnp.dot(parts, moving, preferred_element_type=F32)
+        rows = []
+        for c in range(3):
+            r = 3 * c * blocks + b
+            found = there[r:r + 1] + there[r + blocks:r + blocks + 1]
+            found = found + there[r + 2 * blocks:r + 2 * blocks + 1]
+            row = stiffness_ref[b] * (found - points_ref[c, b:b + 1, :])
+            rows.append(jnp.where(diagonal, jnp.concatenate([row] * k, axis=1), 0.0))
+        rows.append(jnp.zeros_like(rows[0]))
+        lefts.append(jnp.concatenate(rows, axis=0).astype(BF16))
+
+    owner_row = to_row(owners_ref[:, 0, :])
+    places = slot_row(owner_row, to_column(owner_row), devices)
+    total = devices * per_owner
+    chosen = iota((total, places.shape[1]), 0) == places
+    selector = one_hot(chosen)
+
+    for b in range(blocks):
+        wait_block(b)
+        right = loaded_ref[b].reshape(k * points, patch)
+        result = jnp.dot(lefts[b], right, preferred_element_type=F32)
+        for c in range(3):
+            contrib_ref[c, b * k:(b + 1) * k, :] = result[c * k:(c + 1) * k]
+
+    tiles = patch // LANES
+    width = 3 * tiles * per_owner
+    for c in range(3):
+        packed = jnp.dot(selector, contrib_ref[c].astype(BF16), preferred_element_type=F32)
         for p in range(per_owner):
-            table = jnp.where(lane == p, column[p * devices:(p + 1) * devices], table)
-        for d in range(devices):
-            table_ref[d] = table[d:d + 1]
-
-
-def start_swap(rows, columns, ins, outs, send_sem, recv_sem, own_sem):
+            for t in range(tiles):
+                stage_ref[pl.ds(p * 3 * tiles + c * tiles + t, devices, stride=width), :] = (
+                    packed[p * devices:(p + 1) * devices, t * LANES:(t + 1) * LANES]
+                )
+    out_ref[...] = stage_ref[...].reshape(out_ref.shape).astype(BF16)
+    column = jnp.max(jnp.where(chosen, to_row(slots_ref[...]), -1), axis=1, keepdims=True)
+    lane = iota((devices, LANES), 1)
+    table = jnp.full((devices, LANES), -1, I32)
+    for p in range(per_owner):
+        table = jnp.where(lane == p, column[p * devices:(p + 1) * devices], table)
+    for d in range(devices):
+        table_ref[d] = table[d:d + 1]
+
+
+def start_swap(rows, columns, ins, outs, send_sem, recv_sem, own_sem, prepare=None):
     devices = rows * columns
     count = len(ins)
     me = lax.axis_index("gx") * columns + lax.axis_index("gy")
@@ -124,6 +131,8 @@
         return carry
 
     lax.fori_loop(1, devices, hello, 0)
+    if prepare is not None:
+        prepare()
     pl.semaphore_wait(barrier, devices - 1)
 
     def copy(n, off):
@@ -196,10 +205,12 @@
 
 
 def dispatch_kernel(
-    rows_grid, columns_grid, per_owner, out_ref, outtable_ref, velocity_ref,
+    rows_grid, columns_grid, per_owner, points_ref, stiffness_ref, links_ref, owners_ref,
+    slots_ref, weights_ref, velocity_ref,
     received_ref, table_ref, sides_out, ends_out, corners_out,
+    out_ref, outtable_ref, loaded_ref, contrib_ref,
     row_ref, end_ref, edge_ref, ends_ref, stage_ref, force_ref, sides_send, ends_send,
-    corners_send, send_sem, recv_sem, own_sem, load_sem, hsend_sem, hrecv_sem,
+    corners_send, send_sem, recv_sem, own_sem, load_sem, block_sem, hsend_sem, hrecv_sem,
 ):
     devices = rows_grid * columns_grid
     total = devices * per_owner
@@ -214,11 +225,24 @@
         loads.append(pltpu.make_async_copy(
             velocity_ref.at[:, :, :, pl.ds(side * (columns - LANES), LANES)], end_ref.at[side],
             load_sem.at[2 + side]))
+
+    def block(b):
+        return pltpu.make_async_copy(weights_ref.at[b], loaded_ref.at[b], block_sem.at[b])
+
+    for b in range(weights_ref.shape[0]):
+        block(b).start()
     for load in loads:
         load.start()
+
+    def prepare():
+        spread(
+            devices, per_owner, points_ref, stiffness_ref, links_ref, owners_ref, slots_ref,
+            loaded_ref, out_ref, outtable_ref, contrib_ref, stage_ref,
+            lambda b: block(b).wait())
+
     wait = start_swap(
         rows_grid, columns_grid, [out_ref, outtable_ref], [received_ref, table_ref],
-        send_sem, recv_sem, own_sem)
+        send_sem, recv_sem, own_sem, prepare)
 
     cell, want = iota((cells, LANES), 0), iota((cells, LANES), 1)
     z, x = cell // rows, lax.rem(cell, rows)
@@ -390,7 +414,8 @@
     for c in range(3):
         force_ref[c] = (force_step * unpack(stage_ref, devices, per_owner, tiles, c)).astype(BF16)
     slots_row = table_row(table_ref, devices, per_owner)
-    for n in range(chunks):
+
+    def settle(n):
         load(n).wait()
         placing = one_hot(iota((cells, total), 0) + n * cells == slots_row)
         span = slice(n * chunk, (n + 1) * chunk)
@@ -432,7 +457,12 @@
                 second_ref[c, z, 8 * t:8 * t + 8, :] = jnp.where(keep, new[c], 0.0)
         return carry
 
-    lax.fori_loop(0, layers, step_one, 0)
+    settle(0)
+    settle(1)
+    for n in range(2, chunks):
+        settle(n)
+        lax.fori_loop((n - 1) * chunk, n * chunk, step_one, 0)
+    lax.fori_loop(layers - chunk, layers + chunk, lambda z, v: step_one(lax.rem(z, layers), v), 0)
 
     def step_two(z, carry):
         for t in range(rows // 8):
@@ -468,7 +498,7 @@
 
 
 def gather_kernel(
-    rows_grid, columns_grid, per_owner, replies_ref, owners_ref, points_ref, weights_ref,
+    rows_grid, columns_grid, per_owner, replies_ref, owners_ref, weights_ref,
     out_ref, returned_ref, loaded_ref, stage_ref, picked_ref, send_sem, recv_sem, own_sem, load_sem,
 ):
     devices = rows_grid * columns_grid
@@ -507,7 +537,7 @@
             for n in range(1, k):
                 fold = fold + own[:, n * points:(n + 1) * points]
             interp = jnp.sum(fold, axis=0, keepdims=True)
-            out_ref[c, b:b + 1, :] = points_ref[c, b:b + 1, :] + fiber_step * interp
+            out_ref[c, b:b + 1, :] = interp
 
 
 def shards(rows_grid, columns_grid, velocity, fiber_points, stiffness, links, delta_weights,
@@ -522,25 +552,9 @@
     width = 3 * tiles * per_owner
     owners = jnp.transpose(owners, (0, 2, 1))
     points_first = jnp.transpose(fiber_points, (1, 0, 2))
-    whole = lambda shape: pl.BlockSpec(shape, lambda i: (0,) * len(shape))
     message = jax.ShapeDtypeStruct((devices, width, LANES), BF16)
     table_shape = jax.ShapeDtypeStruct((devices, 1, LANES), I32)
     stage = pltpu.VMEM((devices * width, LANES), F32)
-    outgoing, table = pl.pallas_call(
-        functools.partial(spread_kernel, devices, per_owner),
-        grid=(blocks,),
-        out_shape=[message, table_shape],
-        in_specs=[
-            whole(points_first.shape), SMEM, whole(links.shape), whole(owners.shape),
-            whole(patch_slots.shape),
-            pl.BlockSpec((1, intersection, points, patch), lambda b: (b, 0, 0, 0)),
-        ],
-        out_specs=[whole(message.shape), whole(table_shape.shape)],
-        scratch_shapes=[
-            pltpu.VMEM((3, blocks, points), F32), pltpu.VMEM((3, entries, patch), F32), stage,
-        ],
-    )(points_first, stiffness, links, owners, patch_slots, delta_weights)
-
     sides_shape = (2, 3, 2, layers, columns)
     ends_shape = (2, 8, layers * rows)
     received, slots, sides, ends, corners = pl.pallas_call(
@@ -551,9 +565,13 @@
             jax.ShapeDtypeStruct(ends_shape, BF16),
             jax.ShapeDtypeStruct((4, 8, LANES), BF16),
         ],
-        in_specs=[VMEM, VMEM, ANY],
+        in_specs=[VMEM, SMEM, VMEM, VMEM, VMEM, ANY, ANY],
         out_specs=[VMEM] * 5,
         scratch_shapes=[
+            pltpu.VMEM(message.shape, BF16),
+            pltpu.VMEM(table_shape.shape, I32),
+            pltpu.VMEM(delta_weights.shape, BF16),
+            pltpu.VMEM((3, entries, patch), F32),
             pltpu.VMEM((2, 3, layers, 8, columns), F32),
             pltpu.VMEM((2, 3, layers, rows, LANES), F32),
             pltpu.VMEM((layers * rows, LANES), BF16),
@@ -565,11 +583,12 @@
             pltpu.VMEM((2, 8, LANES), BF16),
             *swap_sems(2, devices),
             pltpu.SemaphoreType.DMA((4,)),
+            pltpu.SemaphoreType.DMA((blocks,)),
             pltpu.SemaphoreType.DMA((8,)),
             pltpu.SemaphoreType.DMA((8,)),
         ],
         compiler_params=pltpu.CompilerParams(collective_id=0, has_side_effects=True),
-    )(outgoing, table, velocity)
+    )(points_first, stiffness, links, owners, patch_slots, delta_weights, velocity)
 
     chunk = 8
     extended = (3, layers, rows + 8, columns + LANES)
@@ -587,10 +606,10 @@
         ],
     )(sides, ends, corners, slots, received, velocity)
 
-    moved = pl.pallas_call(
+    interp = pl.pallas_call(
         functools.partial(gather_kernel, rows_grid, columns_grid, per_owner),
         out_shape=jax.ShapeDtypeStruct(points_first.shape, F32),
-        in_specs=[VMEM, VMEM, VMEM, ANY],
+        in_specs=[VMEM, VMEM, ANY],
         out_specs=VMEM,
         scratch_shapes=[
             pltpu.VMEM(message.shape, BF16), pltpu.VMEM(delta_weights.shape, BF16), stage,
@@ -598,8 +617,8 @@
             pltpu.SemaphoreType.DMA((blocks,)),
         ],
         compiler_params=pltpu.CompilerParams(collective_id=1, has_side_effects=True),
-    )(replies, owners, points_first, delta_weights)
-    return fluid, jnp.transpose(moved, (1, 0, 2))
+    )(replies, owners, delta_weights)
+    return fluid, fiber_points + fiber_step * jnp.transpose(interp, (1, 0, 2))
 
 
 def solution(mesh):

time: 79.7 us -> 73.6 us (0.923)
  Pallas kernels: 77.4 us -> 71.4 us
  other arithmetic: 0 us -> 1.31 us
  local copies, waits for them, and re-layouts: 1.31 us -> 0.01 us
    pallas_call x1 -> x0, Pallas kernels: 8.08 us -> none  [shards(): pl.pallas_call(functools.partial(spread_kernel, devices, per_owner), grid...]
    pallas_call x1, Pallas kernels: 24.4 us -> 26.5 us  [shards(): pl.pallas_call(functools.partial(dispatch_kernel, rows_grid, columns_grid...]
    add x0 -> x1, other arithmetic: none -> 1.31 us  [shards(): return (fluid, fiber_points + fiber_step * jnp.transpose(interp, (1, 0, 2)))]
    unnamed x1 -> x2, local copies, waits for them, and re-layouts: 1.31 us -> 0.01 us
where the time goes in v3:
time: 73.6 us; the launch traced here: 73.4 us
  Pallas kernels  71.4 us (97%)
  other arithmetic  1.31 us (2%)
    pallas_call x1, Pallas kernels, shards(): pl.pallas_call(functools.partial(dispatch_kernel, rows_grid, columns_grid...  26.5 us
    pallas_call x1, Pallas kernels, shards(): pl.pallas_call(functools.partial(sweeps_kernel, devices, per_owner, rows_...  23.4 us
    pallas_call x1, Pallas kernels, shards(): pl.pallas_call(functools.partial(gather_kernel, rows_grid, columns_grid,...  21.5 us

profile of v3, /device:TPU:0, one launch (start us, length us, event | category | flops | bytes accessed | tf_op | source)
XLA Modules:
  0.0 73.4 jit_solution(2722909732732294447)
XLA Ops:
  0.6 26.5 %shard_map.86 = (bf16[32,48,128]{2,1,0:T(8,128)(2,1)}, s32[32,1,128]{2,1,0:T(1,128)}, bf16[2,3,2,32,512]{4,3,2,1,0:T(8,128)(2,1)}, bf16[2,8,1024]{2,1,0:T(8,128)(2,1)}, bf16[4,8,128]{2,1,0:T(8,128)(2,1)}) custom-call(f32[3,8,128]{2,1,0:T(8,128)} %bitcast.6, f32[8]{0:T(128)} %stiffness_ref.1, s32[8,128]{1,0:T(8,128)} %links_ref.1, s32[8,1,8]{2,1,0:T(1,128)} %bitcast.7, ...), custom_call_target="tpu_custom_call" | custom-call | tf_op jit(solution)/shard_map/pallas_call | solution.py:560
  27.1 0.0 copy-start
  27.1 23.4 %shard_map.87 = (f32[3,32,32,512]{3,2,1,0:T(8,128)}, bf16[32,48,128]{2,1,0:T(8,128)(2,1)}) custom-call(bf16[2,3,2,32,512]{4,3,2,1,0:T(8,128)(2,1)} %get-tuple-element.9.sides_ref, bf16[2,8,1024]{2,1,0:T(8,128)(2,1)} %get-tuple-element.10.ends_ref, bf16[4,8,128]{2,1,0:T(8,128)(2,1)} %get-tuple-element.11.corners_ref, ...), custom_call_target="tpu_custom_call" | custom-call | tf_op jit(solution)/shard_map/pallas_call | solution.py:595
  50.6 21.5 %shard_map.88 = f32[3,8,128]{2,1,0:T(8,128)} custom-call(bf16[32,48,128]{2,1,0:T(8,128)(2,1)} %get-tuple-element.15.replies_ref, s32[8,1,8]{2,1,0:T(1,128)} %bitcast.8, bf16[8,8,128,512]{3,2,1,0:T(8,128)(2,1)} %weights_ref.3), custom_call_target="tpu_custom_call" | custom-call | tf_op jit(solution)/shard_map/pallas_call | solution.py:609
  72.1 0.0 copy-done
  72.1 1.3 %bitcast_add_fusion = f32[8,3,128]{2,0,1:T(8,128)} fusion(f32[8,3,128]{2,0,1:T(8,128)S(1)} %copy-done, f32[3,8,128]{2,1,0:T(8,128)} %shard_map.88), kind=kLoop, calls=%fused_computation | loop fusion | flops 6144 | bytes 36864 | tf_op jit(solution)/shard_map/add | solution.py:621
Async XLA Ops:
  27.1 44.9 %copy-start = (f32[8,3,128]{2,0,1:T(8,128)S(1)}, f32[8,3,128]{2,0,1:T(8,128)}, u32[]{:S(2)}) copy-start(f32[8,3,128]{2,0,1:T(8,128)} %param.8) | copy-start | bytes 36868

commit v4 on v3

--- a/solution.py
+++ b/solution.py
@@ -356,7 +356,7 @@
 def sweeps_kernel(
     devices, per_owner, rows_grid, columns_grid, chunk, sides_ref, ends_ref, corners_ref,
     table_ref, received_ref, velocity_ref,
-    fluid_ref, replies_ref, first_ref, second_ref, last_ref, side_ref, stage_ref, sum_ref,
+    fluid_ref, sum_ref, first_ref, second_ref, last_ref, side_ref, stage_ref,
     force_ref, in_sem, out_sem,
 ):
     _, layers, rows, columns = velocity_ref.shape
@@ -452,9 +452,14 @@
     def step_one(z, carry):
         for t in range(tall // 8):
             new = sweep(*neighbours(first_ref, z, t, wide))
-            keep = lane_keep if t < rows // 8 else lane_keep & row_keep
             for c in range(3):
-                second_ref[c, z, 8 * t:8 * t + 8, :] = jnp.where(keep, new[c], 0.0)
+                if t < rows // 8:
+                    second_ref[c, z, 8 * t:8 * t + 8, 0:columns] = new[c][:, 0:columns]
+                    second_ref[c, z, 8 * t:8 * t + 8, columns:] = jnp.where(
+                        lane_keep[:, columns:], new[c][:, columns:], 0.0)
+                else:
+                    second_ref[c, z, 8 * t:8 * t + 8, :] = jnp.where(
+                        lane_keep & row_keep, new[c], 0.0)
         return carry
 
     settle(0)
@@ -485,21 +490,13 @@
             flat = last_ref[c, n * chunk:(n + 1) * chunk].reshape(cells, columns).astype(BF16)
             part = jnp.dot(taking, flat, preferred_element_type=F32)
             sum_ref[c] = part if n == 0 else sum_ref[c] + part
-    width = 3 * tiles * per_owner
-    for c in range(3):
-        for p in range(per_owner):
-            for t in range(tiles):
-                stage_ref[pl.ds(p * 3 * tiles + c * tiles + t, devices, stride=width), :] = (
-                    sum_ref[c, p * devices:(p + 1) * devices, t * LANES:(t + 1) * LANES]
-                )
-    replies_ref[...] = stage_ref[...].reshape(replies_ref.shape).astype(BF16)
     for n in range(chunks):
         store(n).wait()
 
 
 def gather_kernel(
     rows_grid, columns_grid, per_owner, replies_ref, owners_ref, weights_ref,
-    out_ref, returned_ref, loaded_ref, stage_ref, picked_ref, send_sem, recv_sem, own_sem, load_sem,
+    out_ref, packed_ref, returned_ref, loaded_ref, stage_ref, picked_ref, send_sem, recv_sem, own_sem, load_sem,
 ):
     devices = rows_grid * columns_grid
     blocks, k, points, patch = weights_ref.shape
@@ -511,8 +508,20 @@
 
     for b in range(blocks):
         load(b).start()
+    width = 3 * tiles * per_owner
+
+    def prepare():
+        for c in range(3):
+            for p in range(per_owner):
+                for t in range(tiles):
+                    stage_ref[pl.ds(p * 3 * tiles + c * tiles + t, devices, stride=width), :] = (
+                        replies_ref[c, p * devices:(p + 1) * devices, t * LANES:(t + 1) * LANES]
+                    )
+        packed_ref[...] = stage_ref[...].reshape(packed_ref.shape).astype(BF16)
+
     wait = start_swap(
-        rows_grid, columns_grid, [replies_ref], [returned_ref], send_sem, recv_sem, own_sem)
+        rows_grid, columns_grid, [packed_ref], [returned_ref], send_sem, recv_sem, own_sem,
+        prepare)
     owner_row = to_row(owners_ref[:, 0, :])
     places = slot_column(owner_row, to_column(owner_row), devices)
     selector = one_hot(iota((places.shape[0], total), 1) == places)
@@ -594,13 +603,16 @@
     extended = (3, layers, rows + 8, columns + LANES)
     fluid, replies = pl.pallas_call(
         functools.partial(sweeps_kernel, devices, per_owner, rows_grid, columns_grid, chunk),
-        out_shape=[jax.ShapeDtypeStruct(velocity.shape, F32), message],
+        out_shape=[
+            jax.ShapeDtypeStruct(velocity.shape, F32),
+            jax.ShapeDtypeStruct((3, total, patch), F32),
+        ],
         in_specs=[VMEM] * 5 + [ANY],
         out_specs=[ANY, VMEM],
         scratch_shapes=[
             pltpu.VMEM(extended, F32), pltpu.VMEM(extended, F32), pltpu.VMEM(velocity.shape, F32),
             pltpu.VMEM((2, 3, 2, layers, columns + LANES), F32), stage,
-            pltpu.VMEM((3, total, patch), F32), pltpu.VMEM((3, total, patch), BF16),
+            pltpu.VMEM((3, total, patch), BF16),
             pltpu.SemaphoreType.DMA((layers // chunk,)),
             pltpu.SemaphoreType.DMA((layers // chunk,)),
         ],
@@ -612,7 +624,8 @@
         in_specs=[VMEM, VMEM, ANY],
         out_specs=VMEM,
         scratch_shapes=[
-            pltpu.VMEM(message.shape, BF16), pltpu.VMEM(delta_weights.shape, BF16), stage,
+            pltpu.VMEM(message.shape, BF16), pltpu.VMEM(message.shape, BF16),
+            pltpu.VMEM(delta_weights.shape, BF16), stage,
             pltpu.VMEM((3, entries, patch), F32), *swap_sems(1, devices),
             pltpu.SemaphoreType.DMA((blocks,)),
         ],

time: 73.6 us -> 73.9 us (level)
  no operation moved by 1% of the time
where the time goes in v4:
time: 73.9 us; the launch traced here: 73.7 us
  Pallas kernels  71.7 us (97%)
  other arithmetic  1.31 us (2%)
    pallas_call x1, Pallas kernels, shards(): pl.pallas_call(functools.partial(dispatch_kernel, rows_grid, columns_grid...  26.5 us
    pallas_call x1, Pallas kernels, shards(): pl.pallas_call(functools.partial(sweeps_kernel, devices, per_owner, rows_...  23.6 us
    pallas_call x1, Pallas kernels, shards(): pl.pallas_call(functools.partial(gather_kernel, rows_grid, columns_grid,...  21.6 us

profile of v4, /device:TPU:0, one launch (start us, length us, event | category | flops | bytes accessed | tf_op | source)
XLA Modules:
  0.0 73.7 jit_solution(11898572763713338164)
XLA Ops:
  0.6 26.5 %shard_map.86 = (bf16[32,48,128]{2,1,0:T(8,128)(2,1)}, s32[32,1,128]{2,1,0:T(1,128)}, bf16[2,3,2,32,512]{4,3,2,1,0:T(8,128)(2,1)}, bf16[2,8,1024]{2,1,0:T(8,128)(2,1)}, bf16[4,8,128]{2,1,0:T(8,128)(2,1)}) custom-call(f32[3,8,128]{2,1,0:T(8,128)} %bitcast.6, f32[8]{0:T(128)} %stiffness_ref.1, s32[8,128]{1,0:T(8,128)} %links_ref.1, s32[8,1,8]{2,1,0:T(1,128)} %bitcast.7, ...), custom_call_target="tpu_custom_call" | custom-call | tf_op jit(solution)/shard_map/pallas_call | solution.py:569
  27.1 23.6 %shard_map.87 = (f32[3,32,32,512]{3,2,1,0:T(8,128)}, f32[3,128,512]{2,1,0:T(8,128)}) custom-call(bf16[2,3,2,32,512]{4,3,2,1,0:T(8,128)(2,1)} %get-tuple-element.9.sides_ref, bf16[2,8,1024]{2,1,0:T(8,128)(2,1)} %get-tuple-element.10.ends_ref, bf16[4,8,128]{2,1,0:T(8,128)(2,1)} %get-tuple-element.11.corners_ref, s32[32,1,128]{2,1,0:T(1,128)} %get-tuple-element.12.table_ref, ...), custom_call_target="tpu_custom_call" | custom-call | tf_op jit(solution)/shard_map/pallas_call | solution.py:604
  50.7 0.0 copy-start
  50.7 21.6 %shard_map.88 = f32[3,8,128]{2,1,0:T(8,128)} custom-call(f32[3,128,512]{2,1,0:T(8,128)} %get-tuple-element.15.replies_ref, s32[8,1,8]{2,1,0:T(1,128)} %bitcast.8, bf16[8,8,128,512]{3,2,1,0:T(8,128)(2,1)} %weights_ref.3), custom_call_target="tpu_custom_call" | custom-call | tf_op jit(solution)/shard_map/pallas_call | solution.py:621
  72.3 0.0 copy-done
  72.4 1.3 %bitcast_add_fusion = f32[8,3,128]{2,0,1:T(8,128)} fusion(f32[8,3,128]{2,0,1:T(8,128)S(1)} %copy-done, f32[3,8,128]{2,1,0:T(8,128)} %shard_map.88), kind=kLoop, calls=%fused_computation | loop fusion | flops 6144 | bytes 36864 | tf_op jit(solution)/shard_map/add | solution.py:634
Async XLA Ops:
  50.7 21.6 %copy-start = (f32[8,3,128]{2,0,1:T(8,128)S(1)}, f32[8,3,128]{2,0,1:T(8,128)}, u32[]{:S(2)}) copy-start(f32[8,3,128]{2,0,1:T(8,128)} %param.8) | copy-start | bytes 36868
